TPU v7x, 32 devices: a whole 2x2x4 slice. The times are simulated.
32 devices in a mesh: seq: 8 (over z, y), leaf: 4 (over x, core).
Axes of the slice: x: 2, y: 2, z: 4, core: 2. Of those that a mesh axis runs over, the one named last changes fastest.
Arguments:
- queries: bfloat16 [6144, 4096], P(('leaf', 'seq')), parts along dimension 0, may hold values from -6 to 6
- key_vectors: bfloat16 [6144, 4096], P(('leaf', 'seq')), parts along dimension 0, may hold values from -0.52734375 to 0.52734375
- value_vectors: bfloat16 [6144, 4096], P(('leaf', 'seq')), parts along dimension 0, may hold values from -6 to 6
- output_grad: bfloat16 [6144, 4096], P(('leaf', 'seq')), parts along dimension 0, may hold values from -6 to 6
- log_decay: float32 [6144, 32], P(('leaf', 'seq')), parts along dimension 0, may hold values from -1 to 0
- norm_gain: float32 [4096], replicated, may hold values from 0.1 to 1.9
- parent: int32 [32], P(('leaf', 'seq')), parts along dimension 0, may hold values from -1 to 6, as said below
- fork_flag: int32 [32], P(('leaf', 'seq')), parts along dimension 0, may hold values from 0 to 1, as said below
Outputs:
- attended: bfloat16 [6144, 4096], P(('leaf', 'seq')), parts along dimension 0
- query_grad: bfloat16 [6144, 4096], P(('leaf', 'seq')), parts along dimension 0
- key_grad: bfloat16 [6144, 4096], P(('leaf', 'seq')), parts along dimension 0
- value_grad: bfloat16 [6144, 4096], P(('leaf', 'seq')), parts along dimension 0
- gain_grad: float32 [16384], P('leaf'), parts along dimension 0
There are 4 independent parts, one for each index of `leaf`. A program takes and returns all parts, laid end to end along the dimension named above; an argument that names none is the same for every part. Nothing has to cross between parts.
Inputs may be any that keep to these rules, and one draw needn't show every extreme that they name: parent[n] is -1 where block n begins a new tree (always block 0), n - 1 where it continues the block before it (always the last block), and n - 2 where it starts a new branch from the branch register. fork_flag[0] is 1 and the last block's flag is 0.
All inputs are finite; a program needn't handle non-finite values.
Results may differ from a plain program's by a relative error of at most 0.0069.
Values may be sent and summed in bfloat16 or wider, within the bound.
No kernel may reach another device: no remote copies, remote signals or barrier semaphores. Data moves between devices by JAX's collectives and lax.ppermute only.
A program may use at most 128 MiB of HBM per device.

v0:
```python
import functools
import jax
import jax.numpy as jnp
from jax import lax
from jax.experimental import pallas as pl
from jax.experimental.pallas import tpu as pltpu
from jax.sharding import PartitionSpec as P

eps = 1e-06
highest = lax.Precision.HIGHEST
f32 = jnp.float32
bf16 = jnp.bfloat16
GROUP = 4
CHUNKS = 2


def dot(a, b, ca, cb):
    return lax.dot_general(a, b, (((ca,), (cb,)), ((), ())), preferred_element_type=f32)


def split3(x):
    hi = x.astype(bf16).astype(f32)
    mid = (x - hi).astype(bf16).astype(f32)
    low = (x - hi - mid).astype(bf16).astype(f32)
    return [hi, mid, low]


def pack_rows(rows, count):
    ids = lax.broadcasted_iota(jnp.int32, (count, rows[0].shape[-1]), 0)
    out = jnp.zeros(ids.shape, f32)
    for r, row in enumerate(rows):
        out = jnp.where(ids == r, row, out)
    return out.astype(bf16)


def column(cum, head):
    ids = lax.broadcasted_iota(jnp.int32, cum.shape, 1)
    return jnp.sum(jnp.where(ids == head, cum, 0.0), axis=1, keepdims=True)


def route(step, source, targets):
    for i, target in enumerate(targets):

        @pl.when(step == i)
        def _(target=target):
            target[...] = source[...]


def fetch(step, sources, target):
    for i, source in enumerate(sources):

        @pl.when(step == i)
        def _(source=source):
            target[...] = source[...]


class Plan:
    def __init__(self, length, heads, width, devices):
        self.length, self.heads, self.width, self.devices = length, heads, width, devices
        self.per = heads // CHUNKS // GROUP
        self.rows = self.per * width
        self.extra = -(-(3 * self.per + 3) // 16) * 16
        self.piece = self.rows + self.extra
        self.cols = self.per * width
        self.chunk_cols = GROUP * self.cols

    def head(self, chunk, step, scal, t):
        return (chunk * GROUP + (step ^ scal[0])) * self.per + t

    def fixed(self, shape):
        return pl.BlockSpec(shape, lambda k, s: (0,) * len(shape))

    def real(self, chunk):
        return pl.BlockSpec((self.length, self.cols), lambda k, s: (0, chunk * GROUP + (k ^ s[0])))

    def rel(self):
        return pl.BlockSpec((self.length, self.cols), lambda k, s: (0, k))

    def pieces(self):
        return [self.fixed((self.piece, self.width))] * GROUP

    def pieces_shape(self):
        return [jax.ShapeDtypeStruct((self.piece, self.width), bf16)] * GROUP


def call(body, name, grid, scal, args, in_specs, outs, out_specs, scratch, flops, moved, aliases=None):
    return pl.pallas_call(
        body,
        name=name,
        out_shape=outs,
        grid_spec=pltpu.PrefetchScalarGridSpec(
            num_scalar_prefetch=1,
            grid=grid,
            in_specs=in_specs,
            out_specs=out_specs,
            scratch_shapes=scratch,
        ),
        input_output_aliases=aliases or {},
        cost_estimate=pl.CostEstimate(flops=flops, bytes_accessed=moved, transcendentals=0),
    )(scal, *args)


def state_body(p, chunk, first, scal, decay, keys, values, *refs):
    outs, refs = refs[:GROUP], refs[GROUP:]
    step = pl.program_id(0)
    if first:
        cum_ref, flip_ref, blk = refs

        @pl.when(step == 0)
        def _():
            rows = lax.broadcasted_iota(jnp.int32, (p.length, p.length), 0)
            cols = lax.broadcasted_iota(jnp.int32, (p.length, p.length), 1)
            tri = (rows >= cols).astype(f32)
            dims = (((1,), (0,)), ((), ()))
            cum_ref[...] = lax.dot_general(tri, decay[...], dims, precision=highest, preferred_element_type=f32)
            flip_ref[...] = jnp.transpose(cum_ref[...])

    else:
        cum_ref, blk = decay, refs[0]
    cum = cum_ref[...]
    marks = []
    for t in range(p.per):
        at = slice(t * p.width, (t + 1) * p.width)
        col = column(cum, p.head(chunk, step, scal, t))
        last = col[p.length - 1 : p.length]
        scaled = (keys[:, at].astype(f32) * jnp.exp(last - col)).astype(bf16)
        blk[at, :] = dot(scaled, values[:, at], 0, 0).astype(bf16)
        marks += split3(jnp.broadcast_to(jnp.exp(last), (1, p.width)))
    for j in (1, 2, 3):
        marks.append(jnp.full((1, p.width), scal[j].astype(f32)))
    blk[p.rows :, :] = pack_rows(marks, p.extra)
    route(step, blk, outs)


def state_call(p, chunk, scal, decay, keys, values):
    first = chunk == 0
    n = p.length
    outs, out_specs = p.pieces_shape(), p.pieces()
    if first:
        outs = outs + [jax.ShapeDtypeStruct((n, p.heads), f32), jax.ShapeDtypeStruct((p.heads, n), f32)]
        out_specs = out_specs + [p.fixed((n, p.heads)), p.fixed((p.heads, n))]
    return call(
        functools.partial(state_body, p, chunk, first), f"state{chunk}", (GROUP,), scal,
        (decay, keys, values),
        [p.fixed((n, p.heads)), p.real(chunk), p.real(chunk)],
        outs, out_specs,
        [pltpu.VMEM((p.piece, p.width), bf16)],
        2 * n * p.width * p.chunk_cols, 4 * n * p.chunk_cols + 2 * GROUP * p.piece * p.width,
    )


def mask_of(p, cum, flip, head):
    rows = lax.broadcasted_iota(jnp.int32, (p.length, p.length), 0)
    cols = lax.broadcasted_iota(jnp.int32, (p.length, p.length), 1)
    diff = column(cum[...], head) - flip[pl.ds(head, 1), :]
    return jnp.exp(jnp.where(rows >= cols, diff, -jnp.inf))


def within_body(p, chunk, scal, cum, flip, queries, keys, values, within, weights):
    step = pl.program_id(0)
    for t in range(p.per):
        at = slice(t * p.width, (t + 1) * p.width)
        mask = mask_of(p, cum, flip, p.head(chunk, step, scal, t))
        weighted = (dot(queries[:, at], keys[:, at], 1, 1) * mask).astype(bf16)
        weights[t] = weighted
        within[:, at] = dot(weighted, values[:, at], 1, 0)


def within_call(p, chunk, scal, cum, flip, queries, keys, values):
    n = p.length
    return call(
        functools.partial(within_body, p, chunk), f"within{chunk}", (GROUP,), scal,
        (cum, flip, queries, keys, values),
        [p.fixed((n, p.heads)), p.fixed((p.heads, n)), p.real(chunk), p.real(chunk), p.real(chunk)],
        [jax.ShapeDtypeStruct((n, p.chunk_cols), f32), jax.ShapeDtypeStruct((GROUP * p.per, n, n), bf16)],
        [p.rel(), pl.BlockSpec((p.per, n, n), lambda k, s: (k, 0, 0))],
        [],
        4 * n * n * p.chunk_cols, 12 * n * p.chunk_cols,
    )


def gather_pieces(scal, refs, target):
    for k, ref in enumerate(refs):
        target[k ^ scal[0]] = ref[...]


def three(ref, n, row):
    parts = ref[n, pl.ds(row, 3), :].astype(f32)
    return parts[0:1] + parts[1:2] + parts[2:3]


def load_marks(p, marks, base, n, t):
    decay = sum(marks[n, base + 3 * t + j : base + 3 * t + j + 1, :].astype(f32) for j in range(3))
    at = base + 3 * p.per
    flag, alpha, beta = (marks[n, at + j : at + j + 1, :].astype(f32) for j in range(3))
    return decay, flag, alpha, beta


def forward_scan(p, start, scr, t, emit):
    branch, state = start
    at = slice(t * p.width, (t + 1) * p.width)
    for n in range(GROUP):
        decay, flag, alpha, beta = load_marks(p, scr, p.rows, n, t)
        entering = alpha * state + beta * branch
        if emit is not None:
            emit(n, at, entering)
        state = decay * entering + scr[n, at, :].astype(f32)
        branch = flag * state + (1.0 - flag) * branch
    return branch, state


def backward_scan(p, start, scr, marks, t, emit):
    branch, state = start
    at = slice(t * p.width, (t + 1) * p.width)
    for n in reversed(range(GROUP)):
        decay, flag, alpha, beta = load_marks(p, marks, 0, n, t)
        leaving = state + flag * branch
        if emit is not None:
            emit(n, at, leaving)
        through = decay * leaving + scr[n, at, :].astype(f32)
        branch, state = (1.0 - flag) * branch + beta * through, alpha * through
    return branch, state


def zero_pair(p):
    zero = jnp.zeros((p.width, p.width), f32)
    return zero, zero


def edge_body(p, scal, p0, p1, p2, p3, edge, scr):
    gather_pieces(scal, (p0, p1, p2, p3), scr)
    for t in range(p.per):
        branch, state = forward_scan(p, zero_pair(p), scr, t, None)
        edge[0, t * p.width : (t + 1) * p.width, :] = branch.astype(bf16)
        edge[1, t * p.width : (t + 1) * p.width, :] = state.astype(bf16)


def whole(shape):
    return pl.BlockSpec(shape, lambda k, s: (0,) * len(shape))


def edge_call(p, chunk, scal, pieces):
    return call(
        functools.partial(edge_body, p), f"edge{chunk}", (1,), scal, pieces,
        p.pieces(),
        jax.ShapeDtypeStruct((2, p.rows, p.width), bf16), whole((2, p.rows, p.width)),
        [pltpu.VMEM((GROUP, p.piece, p.width), bf16)],
        40 * p.rows * p.width, 12 * p.rows * p.width,
    )


def enter_body(p, scal, p0, p1, p2, p3, coming, o0, o1, o2, o3, scr, out):
    gather_pieces(scal, (p0, p1, p2, p3), scr)
    for t in range(p.per):
        at = slice(t * p.width, (t + 1) * p.width)
        start = (coming[0, at, :].astype(f32), coming[1, at, :].astype(f32))

        def emit(n, at, value):
            out[n, at, :] = value.astype(bf16)

        forward_scan(p, start, scr, t, emit)
    for k, ref in enumerate((o0, o1, o2, o3)):
        ref[...] = out[k ^ scal[0]]


def enter_call(p, chunk, scal, pieces, coming):
    return call(
        functools.partial(enter_body, p), f"enter{chunk}", (1,), scal, (*pieces, coming),
        p.pieces() + [whole((2, p.rows, p.width))],
        [jax.ShapeDtypeStruct((p.rows, p.width), bf16)] * GROUP,
        [whole((p.rows, p.width))] * GROUP,
        [pltpu.VMEM((GROUP, p.piece, p.width), bf16), pltpu.VMEM((GROUP, p.rows, p.width), bf16)],
        60 * p.rows * p.width, 20 * p.rows * p.width,
    )


def norm_body(p, chunk, scal, *refs):
    cum, within, queries, grads, gain, s0, s1, s2, s3 = refs[:9]
    refs = refs[9 + (chunk > 0) :]
    attended, grad_b = refs[0], refs[1]
    outs, blk, state = refs[2 : 2 + GROUP], refs[2 + GROUP], refs[3 + GROUP]
    step = pl.program_id(0)
    fetch(step, (s0, s1, s2, s3), state)
    marks = []
    for t in range(p.per):
        at = slice(t * p.width, (t + 1) * p.width)
        rise = jnp.exp(column(cum[...], p.head(chunk, step, scal, t)))
        scaled = (queries[:, at].astype(f32) * rise).astype(bf16)
        attention = within[:, at] + dot(scaled, state[at, :], 1, 0)
        scale = lax.rsqrt(jnp.mean(attention * attention, axis=-1, keepdims=True) + eps)
        normed = attention * scale
        gain_row = gain[:, at]
        attended[:, at] = (normed * gain_row).astype(bf16)
        out_grad = grads[:, at].astype(f32)
        part = out_grad * gain_row
        pull = jnp.mean(part * normed, axis=-1, keepdims=True)
        grad = ((part - normed * pull) * scale).astype(bf16)
        grad_b[:, at] = grad
        blk[at, :] = dot(scaled, grad, 0, 0).astype(bf16)
        marks += split3(jnp.sum(out_grad * normed, axis=0, keepdims=True))
    blk[p.rows :, :] = pack_rows(marks, p.extra)
    route(step, blk, outs)


def norm_call(p, chunk, scal, cum, within, queries, grads, gain, states, attended):
    n = p.length
    args = (cum, within, queries, grads, gain, *states)
    specs = [p.fixed((n, p.heads)), p.rel(), p.real(chunk), p.real(chunk)]
    specs.append(pl.BlockSpec((1, p.cols), lambda k, s: (0, chunk * GROUP + (k ^ s[0]))))
    specs += [p.fixed((p.rows, p.width))] * GROUP
    aliases = None
    if chunk > 0:
        aliases = {1 + len(args): 0}
        args += (attended,)
        specs.append(pl.BlockSpec(memory_space=pl.ANY))
    full = jax.ShapeDtypeStruct((n, p.heads * p.width), bf16)
    return call(
        functools.partial(norm_body, p, chunk), f"norm{chunk}", (GROUP,), scal, args, specs,
        [full, jax.ShapeDtypeStruct((n, p.chunk_cols), bf16)] + p.pieces_shape(),
        [p.real(chunk), p.rel()] + p.pieces(),
        [pltpu.VMEM((p.piece, p.width), bf16), pltpu.VMEM((p.rows, p.width), bf16)],
        4 * n * p.width * p.chunk_cols, 12 * n * p.chunk_cols, aliases,
    )


def local_body(p, chunk, scal, *refs):
    cum, flip, queries, keys, values, grad_b, weights, s0, s1, s2, s3 = refs[:11]
    query_grad, key_local, value_local, state = refs[11 + (chunk > 0) :]
    step = pl.program_id(0)
    fetch(step, (s0, s1, s2, s3), state)
    for t in range(p.per):
        at = slice(t * p.width, (t + 1) * p.width)
        head = p.head(chunk, step, scal, t)
        mask = mask_of(p, cum, flip, head)
        grad = grad_b[:, at]
        grad_weights = (dot(grad, values[:, at], 1, 1) * mask).astype(bf16)
        rise = jnp.exp(column(cum[...], head))
        query_grad[:, at] = (
            dot(grad_weights, keys[:, at], 1, 0) + rise * dot(grad, state[at, :], 1, 1)
        ).astype(bf16)
        key_local[:, at] = dot(grad_weights, queries[:, at], 0, 0)
        value_local[:, at] = dot(weights[t], grad, 0, 0)


def local_call(p, chunk, scal, cum, flip, queries, keys, values, grad_b, weights, states, query_grad):
    n = p.length
    args = (cum, flip, queries, keys, values, grad_b, weights, *states)
    specs = [p.fixed((n, p.heads)), p.fixed((p.heads, n)), p.real(chunk), p.real(chunk), p.real(chunk)]
    specs += [p.rel(), pl.BlockSpec((p.per, n, n), lambda k, s: (k, 0, 0))]
    specs += [p.fixed((p.rows, p.width))] * GROUP
    aliases = None
    if chunk > 0:
        aliases = {1 + len(args): 0}
        args += (query_grad,)
        specs.append(pl.BlockSpec(memory_space=pl.ANY))
    return call(
        functools.partial(local_body, p, chunk), f"local{chunk}", (GROUP,), scal, args, specs,
        [jax.ShapeDtypeStruct((n, p.heads * p.width), bf16)]
        + [jax.ShapeDtypeStruct((n, p.chunk_cols), f32)] * 2,
        [p.real(chunk), p.rel(), p.rel()],
        [pltpu.VMEM((p.rows, p.width), bf16)],
        10 * n * n * p.chunk_cols, 20 * n * p.chunk_cols, aliases,
    )


def gather_marks(scal, refs, target):
    for k, ref in enumerate(refs):
        target[k ^ scal[0]] = ref[...]


def mark_specs(p):
    at = p.rows // p.extra
    return [pl.BlockSpec((p.extra, p.width), lambda k, s: (at, 0))] * GROUP


def back_edge_body(p, scal, *refs):
    pulls, marks_in, (edge, gain_sum, scr, marks) = refs[:GROUP], refs[GROUP : 2 * GROUP], refs[2 * GROUP :]
    gather_pieces(scal, pulls, scr)
    gather_marks(scal, marks_in, marks)
    for t in range(p.per):
        branch, state = backward_scan(p, zero_pair(p), scr, marks, t, None)
        edge[0, t * p.width : (t + 1) * p.width, :] = branch.astype(bf16)
        edge[1, t * p.width : (t + 1) * p.width, :] = state.astype(bf16)
    gain = jnp.zeros(gain_sum.shape, f32)
    ids = lax.broadcasted_iota(jnp.int32, gain.shape, 0)
    for t in range(p.per):
        row = 0.0
        for n in range(GROUP):
            for j in range(3):
                at = p.rows + 3 * t + j
                row = row + scr[n, at : at + 1, :].astype(f32)
        gain = jnp.where(ids == t, row, gain)
    gain_sum[...] = gain


def back_edge_call(p, chunk, scal, pulls, pieces):
    wide = -(-p.per // 8) * 8
    return call(
        functools.partial(back_edge_body, p), f"back_edge{chunk}", (1,), scal, (*pulls, *pieces),
        p.pieces() + mark_specs(p),
        [jax.ShapeDtypeStruct((2, p.rows, p.width), bf16), jax.ShapeDtypeStruct((wide, p.width), f32)],
        [whole((2, p.rows, p.width)), whole((wide, p.width))],
        [pltpu.VMEM((GROUP, p.piece, p.width), bf16), pltpu.VMEM((GROUP, p.extra, p.width), bf16)],
        40 * p.rows * p.width, 12 * p.rows * p.width,
    )


def leave_body(p, scal, *refs):
    pulls, marks_in, refs = refs[:GROUP], refs[GROUP : 2 * GROUP], refs[2 * GROUP :]
    coming, gain_mine, gain_other = refs[:3]
    outs, (scr, marks, out) = refs[3 : 3 + GROUP], refs[3 + GROUP :]
    gather_pieces(scal, pulls, scr)
    gather_marks(scal, marks_in, marks)
    for t in range(p.per):
        at = slice(t * p.width, (t + 1) * p.width)
        start = (coming[0, at, :].astype(f32), coming[1, at, :].astype(f32))

        def emit(n, at, value):
            out[n, at, :] = value.astype(bf16)

        backward_scan(p, start, scr, marks, t, emit)
    total = gain_mine[...] + gain_other[...]
    rows = []
    for t in range(p.per):
        rows += split3(total[t : t + 1])
    tail = pack_rows(rows, p.extra)
    for k, ref in enumerate(outs):
        ref[: p.rows, :] = out[k ^ scal[0]]
        ref[p.rows :, :] = tail


def leave_call(p, chunk, scal, pulls, pieces, coming, gain_mine, gain_other):
    return call(
        functools.partial(leave_body, p), f"leave{chunk}", (1,), scal,
        (*pulls, *pieces, coming, gain_mine, gain_other),
        p.pieces() + mark_specs(p) + [whole((2, p.rows, p.width))] + [whole(gain_mine.shape)] * 2,
        p.pieces_shape(), p.pieces(),
        [
            pltpu.VMEM((GROUP, p.piece, p.width), bf16),
            pltpu.VMEM((GROUP, p.extra, p.width), bf16),
            pltpu.VMEM((GROUP, p.rows, p.width), bf16),
        ],
        60 * p.rows * p.width, 20 * p.rows * p.width,
    )


def final_body(p, chunk, scal, *refs):
    cum, keys, values, key_local, value_local, s0, s1, s2, s3 = refs[:9]
    key_grad, value_grad, gain_out, state = refs[9 + 2 * (chunk > 0) :]
    step = pl.program_id(0)
    fetch(step, (s0, s1, s2, s3), state)
    gains = []
    for t in range(p.per):
        at = slice(t * p.width, (t + 1) * p.width)
        col = column(cum[...], p.head(chunk, step, scal, t))
        fall = jnp.exp(col[p.length - 1 : p.length] - col)
        scaled_key = (keys[:, at].astype(f32) * fall).astype(bf16)
        scaled_value = (values[:, at].astype(f32) * fall).astype(bf16)
        key_grad[:, at] = (key_local[:, at] + dot(scaled_value, state[at, :], 1, 1)).astype(bf16)
        value_grad[:, at] = (value_local[:, at] + dot(scaled_key, state[at, :], 1, 0)).astype(bf16)
        base = p.rows + 3 * t
        gain_out[step ^ scal[0], t : t + 1, :] = sum(
            state[base + j : base + j + 1, :].astype(f32) for j in range(3)
        )


def final_call(p, chunk, scal, cum, keys, values, key_local, value_local, states, key_grad, value_grad):
    n = p.length
    args = (cum, keys, values, key_local, value_local, *states)
    specs = [p.fixed((n, p.heads)), p.real(chunk), p.real(chunk), p.rel(), p.rel()] + p.pieces()
    aliases = None
    if chunk > 0:
        aliases = {1 + len(args): 0, 2 + len(args): 1}
        args += (key_grad, value_grad)
        specs += [pl.BlockSpec(memory_space=pl.ANY)] * 2
    full = jax.ShapeDtypeStruct((n, p.heads * p.width), bf16)
    return call(
        functools.partial(final_body, p, chunk), f"final{chunk}", (GROUP,), scal, args, specs,
        [full, full, jax.ShapeDtypeStruct((GROUP, p.per, p.width), f32)],
        [p.real(chunk), p.real(chunk), p.fixed((GROUP, p.per, p.width))],
        [pltpu.VMEM((p.piece, p.width), bf16)],
        4 * n * p.width * p.chunk_cols, 16 * n * p.chunk_cols, aliases,
    )


def exchange(p, pieces):
    out = [pieces[0]]
    for k in range(1, GROUP):
        pairs = [(i, i ^ k) for i in range(p.devices)]
        out.append(lax.ppermute(pieces[k], "seq", pairs))
    return out


def shift(p, x, groups):
    pairs = [(i, i + GROUP * groups) for i in range(p.devices) if 0 <= i + GROUP * groups < p.devices]
    return lax.ppermute(x, "seq", pairs)


def group_matrix(p, scal, pieces):
    marks = jnp.stack([piece[p.rows :, 0] for piece in pieces]).astype(f32)
    marks = marks[jnp.arange(GROUP) ^ scal[0]]
    at = 3 * p.per
    decay = marks[:, :at].reshape(GROUP, p.per, 3).sum(-1)
    flag, alpha, beta = (marks[:, at + j : at + j + 1] for j in range(3))
    top = jnp.stack([1.0 - flag + flag * decay * beta, flag * decay * alpha], axis=-1)
    low = jnp.stack([decay * beta, decay * alpha], axis=-1)
    coef = jnp.stack([top, low], axis=2)
    total = coef[0]
    for n in range(1, GROUP):
        total = jnp.einsum("hab,hbc->hac", coef[n], total, precision=highest)
    return total


def across(p, edge, matrix, sign):
    groups = p.devices // GROUP
    if groups <= 2:
        return shift(p, edge, sign)
    shape = (2, p.per, p.width, p.width)
    carry = shift(p, edge, sign).astype(f32).reshape(shape)
    moved = shift(p, matrix, sign)
    reach = 1
    while reach < groups - 1:
        carry_far = shift(p, carry, sign * reach)
        moved_far = shift(p, moved, sign * reach)
        carry = carry + jnp.einsum("hab,bhxy->ahxy", moved, carry_far, precision=highest)
        moved = jnp.einsum("hab,hbc->hac", moved, moved_far, precision=highest)
        reach *= 2
    return carry.astype(bf16).reshape(edge.shape)


def other_gain(p, gain):
    groups = p.devices // GROUP
    if groups == 2:
        return lax.ppermute(gain, "seq", [(i, i ^ GROUP) for i in range(p.devices)])
    same = [[g * GROUP + q for g in range(groups)] for q in range(GROUP)]
    return lax.psum(gain, "seq", axis_index_groups=same) - gain


def on_device(
    queries, key_vectors, value_vectors, output_grad, log_decay, norm_gain, parent, fork_flag
):
    length, heads = log_decay.shape
    width = queries.shape[1] // heads
    p = Plan(length, heads, width, lax.axis_size("seq"))
    position = lax.axis_index("seq").astype(jnp.int32)
    parent_id = parent[0]
    alpha = (parent_id == position - 1).astype(jnp.int32)
    beta = ((parent_id >= 0) & (parent_id != position - 1)).astype(jnp.int32)
    scal = jnp.stack([position % GROUP, fork_flag[0], alpha, beta])
    gain = norm_gain.reshape(1, heads * width)
    chunks = range(CHUNKS)
    many = p.devices // GROUP > 2
    pieces, withins, weights = [None] * CHUNKS, [None] * CHUNKS, [None] * CHUNKS
    cum = flip = None
    for c in chunks:
        if c == 0:
            *sent, cum, flip = state_call(p, c, scal, log_decay, key_vectors, value_vectors)
        else:
            sent = state_call(p, c, scal, cum, key_vectors, value_vectors)
        pieces[c] = exchange(p, sent)
    for c in chunks:
        withins[c], weights[c] = within_call(p, c, scal, cum, flip, queries, key_vectors, value_vectors)
    attended = query_grad = key_grad = value_grad = None
    states, pulls, locals_, matrices = [], [], [], []
    for c in chunks:
        matrices.append(group_matrix(p, scal, pieces[c]) if many else None)
        edge = edge_call(p, c, scal, pieces[c])
        coming = across(p, edge, matrices[c], 1)
        states.append(exchange(p, enter_call(p, c, scal, pieces[c], coming)))
    for c in chunks:
        attended, grad_b, *sent = norm_call(
            p, c, scal, cum, withins[c], queries, output_grad, gain, states[c], attended
        )
        pulls.append(exchange(p, sent))
        query_grad, key_local, value_local = local_call(
            p, c, scal, cum, flip, queries, key_vectors, value_vectors, grad_b, weights[c], states[c], query_grad
        )
        locals_.append((key_local, value_local))
    gains = []
    for c in chunks:
        edge, gain_mine = back_edge_call(p, c, scal, pulls[c], pieces[c])
        flipped = jnp.swapaxes(matrices[c], 1, 2) if many else None
        coming = across(p, edge, flipped, -1)
        sent = leave_call(p, c, scal, pulls[c], pieces[c], coming, gain_mine, other_gain(p, gain_mine))
        back = exchange(p, sent)
        key_grad, value_grad, gain_c = final_call(
            p, c, scal, cum, key_vectors, value_vectors, *locals_[c], back, key_grad, value_grad
        )
        gains.append(gain_c.reshape(-1))
    return attended, query_grad, key_grad, value_grad, jnp.concatenate(gains)


def solution(mesh):
    rows = P(("leaf", "seq"), None)
    flat = P(("leaf", "seq"))
    return jax.shard_map(
        on_device,
        mesh=mesh,
        in_specs=(rows, rows, rows, rows, rows, P(), flat, flat),
        out_specs=(rows, rows, rows, rows, P("leaf")),
        check_vma=False,
    )
```

profile of v0, /device:TPU:0, one launch (start us, length us, event | category | flops | bytes accessed | tf_op | source)
XLA Modules:
  0.0 176.5 jit_solution(17635468635543793079)
XLA Ops:
  1.9 1.5 copy.17.decay
  3.4 0.6 pad_add_fusion.scal
  4.0 5.5 %state0.1 = (bf16[528,128]{1,0:T(8,128)(2,1)}, bf16[528,128]{1,0:T(8,128)(2,1)}, bf16[528,128]{1,0:T(8,128)(2,1)}, bf16[528,128]{1,0:T(8,128)(2,1)}, f32[192,32]{1,0:T(8,128)}, /*index=5*/f32[32,192]{1,0:T(8,128)}) custom-call(s32[4]{0:T(128)} %pad_add_fusion.scal, f32[192,32]{1,0:T(8,128)} %copy.17.decay, bf16[192,4096]{1,0:T(8,128)(2,1)} %refs_1_.3, ...), custom_call_target="tpu_custom_call" | custom-call | flops 100663296 | bytes 2113536 | tf_op jit(solution)/shard_map/state0/pallas_call | solution.py:87
  9.5 3.0 %collective-permute-start.7 = (bf16[528,128]{1,0:T(8,128)(2,1)}, bf16[528,128]{1,0:T(8,128)(2,1)S(1)}, u32[]{:S(2)}, u32[]{:S(2)}) collective-permute-start(bf16[528,128]{1,0:T(8,128)(2,1)} %get-tuple-element.76), channel_id=1, source_target_pairs={{0,4},{4,0},{8,12},{12,8},{16,20},{20,16},{24,28},{28,24},{1,5},{5... | collective-permute-start | bytes 405512 | tf_op jit(solution)/shard_map/ppermute | solution.py:490
  12.6 1.6 collective-permute-start.8
  14.1 5.0 %state1.1 = (bf16[528,128]{1,0:T(8,128)(2,1)}, bf16[528,128]{1,0:T(8,128)(2,1)}, bf16[528,128]{1,0:T(8,128)(2,1)}, bf16[528,128]{1,0:T(8,128)(2,1)}) custom-call(s32[4]{0:T(128)} %pad_add_fusion.scal, f32[192,32]{1,0:T(8,128)} %get-tuple-element.63.cum.decay.refs_0_, bf16[192,4096]{1,0:T(8,128)(2,1)} %refs_1_.3, bf16[192,4096]{1,0:T(8,128)(2,1)} %refs_2_.11), custom_call_target="tpu_custom_call" | custom-call | flops 100663296 | bytes 2113536 | tf_op jit(solution)/shard_map/state1/pallas_call | solution.py:87
  19.2 1.9 %collective-permute-start = (bf16[528,128]{1,0:T(8,128)(2,1)}, bf16[528,128]{1,0:T(8,128)(2,1)S(1)}, u32[]{:S(2)}, u32[]{:S(2)}) collective-permute-start(bf16[528,128]{1,0:T(8,128)(2,1)} %get-tuple-element.67), channel_id=1, source_target_pairs={{0,4},{4,0},{8,12},{12,8},{16,20},{20,16},{24,28},{28,24},{1,5},{5... | collective-permute-start | bytes 405512 | tf_op jit(solution)/shard_map/ppermute | solution.py:490
  21.1 1.6 collective-permute-start.1
  22.7 0.6 copy-done.3
  23.4 0.1 copy-done.5
  23.4 2.8 %edge0.1 = bf16[2,512,128]{2,1,0:T(8,128)(2,1)} custom-call(s32[4]{0:T(128)} %pad_add_fusion.scal, bf16[528,128]{1,0:T(8,128)(2,1)} %get-tuple-element.75.p0.refs_4_, bf16[528,128]{1,0:T(8,128)(2,1)} %copy-done.3, bf16[528,128]{1,0:T(8,128)(2,1)} %copy-done.4, bf16[528,128]{1,0:T(8,128)(2,1)} %copy-done.5), custom_call_target="tpu_custom_call" | custom-call | flops 2621440 | bytes 786432 | tf_op jit(solution)/shard_map/edge0/pallas_call | solution.py:87
  26.2 4.8 %collective-permute-start.10 = (bf16[2,512,128]{2,1,0:T(8,128)(2,1)}, bf16[2,512,128]{2,1,0:T(8,128)(2,1)S(1)}, u32[]{:S(2)}, u32[]{:S(2)}) collective-permute-start(bf16[2,512,128]{2,1,0:T(8,128)(2,1)} %edge0.1), channel_id=1, source_target_pairs={{0,16},{4,20},{8,24},{12,28},{1,17},{5,21},{9,25},{13,29},{2,18},{... | collective-permute-start | bytes 786440 | tf_op jit(solution)/shard_map/ppermute | solution.py:496
  31.2 0.6 copy-done
  31.9 2.8 %edge1.1 = bf16[2,512,128]{2,1,0:T(8,128)(2,1)} custom-call(s32[4]{0:T(128)} %pad_add_fusion.scal, bf16[528,128]{1,0:T(8,128)(2,1)} %get-tuple-element.66.p0.refs_4_, bf16[528,128]{1,0:T(8,128)(2,1)} %copy-done, bf16[528,128]{1,0:T(8,128)(2,1)} %copy-done.1, bf16[528,128]{1,0:T(8,128)(2,1)} %copy-done.2), custom_call_target="tpu_custom_call" | custom-call | flops 2621440 | bytes 786432 | tf_op jit(solution)/shard_map/edge1/pallas_call | solution.py:87
  34.7 2.4 %collective-permute-start.3 = (bf16[2,512,128]{2,1,0:T(8,128)(2,1)}, bf16[2,512,128]{2,1,0:T(8,128)(2,1)S(1)}, u32[]{:S(2)}, u32[]{:S(2)}) collective-permute-start(bf16[2,512,128]{2,1,0:T(8,128)(2,1)} %edge1.1), channel_id=1, source_target_pairs={{0,16},{4,20},{8,24},{12,28},{1,17},{5,21},{9,25},{13,29},{2,18},{... | collective-permute-start | bytes 786440 | tf_op jit(solution)/shard_map/ppermute | solution.py:496
  37.1 0.7 copy-done.21
  37.8 3.1 %enter0.1 = (bf16[512,128]{1,0:T(8,128)(2,1)}, bf16[512,128]{1,0:T(8,128)(2,1)}, bf16[512,128]{1,0:T(8,128)(2,1)}, bf16[512,128]{1,0:T(8,128)(2,1)}) custom-call(s32[4]{0:T(128)} %pad_add_fusion.scal, bf16[528,128]{1,0:T(8,128)(2,1)} %get-tuple-element.75.p0.refs_4_, bf16[528,128]{1,0:T(8,128)(2,1)} %copy-done.3, bf16[528,128]{1,0:T(8,128)(2,1)} %copy-done.4, ...), custom_call_target="tpu_custom_call" | custom-call | flops 3932160 | bytes 1310720 | tf_op jit(solution)/shard_map/enter0/pallas_call | solution.py:87
  40.9 0.7 collective-permute-start.11
  41.6 11.8 %collective-permute-start.12 = (bf16[512,128]{1,0:T(8,128)(2,1)}, bf16[512,128]{1,0:T(8,128)(2,1)S(1)}, u32[]{:S(2)}, u32[]{:S(2)}) collective-permute-start(bf16[512,128]{1,0:T(8,128)(2,1)} %get-tuple-element.81), channel_id=1, source_target_pairs={{0,8},{4,12},{8,0},{12,4},{16,24},{20,28},{24,16},{28,20},{1,9},{5... | collective-permute-start | bytes 393224 | tf_op jit(solution)/shard_map/ppermute | solution.py:490
  53.4 0.7 copy-done.20
  54.1 3.0 %enter1.1 = (bf16[512,128]{1,0:T(8,128)(2,1)}, bf16[512,128]{1,0:T(8,128)(2,1)}, bf16[512,128]{1,0:T(8,128)(2,1)}, bf16[512,128]{1,0:T(8,128)(2,1)}) custom-call(s32[4]{0:T(128)} %pad_add_fusion.scal, bf16[528,128]{1,0:T(8,128)(2,1)} %get-tuple-element.66.p0.refs_4_, bf16[528,128]{1,0:T(8,128)(2,1)} %copy-done, bf16[528,128]{1,0:T(8,128)(2,1)} %copy-done.1, ...), custom_call_target="tpu_custom_call" | custom-call | flops 3932160 | bytes 1310720 | tf_op jit(solution)/shard_map/enter1/pallas_call | solution.py:87
  57.1 1.5 collective-permute-start.4
  58.6 6.0 %within0.1 = (f32[192,2048]{1,0:T(8,128)}, bf16[16,192,192]{2,1,0:T(8,128)(2,1)}) custom-call(s32[4]{0:T(128)} %pad_add_fusion.scal, f32[192,32]{1,0:T(8,128)} %get-tuple-element.63.cum.decay.refs_0_, f32[32,192]{1,0:T(8,128)} %get-tuple-element.64.flip.refs_1_, bf16[192,4096]{1,0:T(8,128)(2,1)} %refs_2_.9, bf16[192,4096]{1,0:T(8,128)(2,1)} %refs_1_.3, ...), custom_call_target="tpu_custom_call" | custom-call | flops 301989888 | bytes 4718592 | tf_op jit(solution)/shard_map/within0/pallas_call | solution.py:87
  64.6 2.1 %collective-permute-start.5 = (bf16[512,128]{1,0:T(8,128)(2,1)S(1)}, bf16[512,128]{1,0:T(8,128)(2,1)S(1)}, u32[]{:S(2)}, u32[]{:S(2)}) collective-permute-start(bf16[512,128]{1,0:T(8,128)(2,1)S(1)} %copy-done.32), channel_id=1, source_target_pairs={{0,8},{4,12},{8,0},{12,4},{16,24},{20,28},{24,16},{28,20},{1,9},{5... | collective-permute-start | bytes 393224 | tf_op jit(solution)/shard_map/ppermute | solution.py:490
  66.7 0.1 collective-permute-start.6
  66.8 0.5 copy-done.12
  67.4 0.1 copy-done.13
  67.5 7.6 %norm0.1 = (bf16[192,4096]{1,0:T(8,128)(2,1)}, bf16[192,2048]{1,0:T(8,128)(2,1)}, bf16[528,128]{1,0:T(8,128)(2,1)}, bf16[528,128]{1,0:T(8,128)(2,1)}, bf16[528,1...) custom-call(s32[4]{0:T(128)} %pad_add_fusion.scal, f32[192,32]{1,0:T(8,128)} %get-tuple-element.63.cum.decay.refs_0_, ...), custom_call_target="tpu_custom_call" | custom-call | flops 201326592 | bytes 4718592 | tf_op jit(solution)/shard_map/norm0/pallas_call | solution.py:87
  75.2 1.5 collective-permute-start.22
  76.7 2.0 %collective-permute-start.23 = (bf16[528,128]{1,0:T(8,128)(2,1)}, bf16[528,128]{1,0:T(8,128)(2,1)S(1)}, u32[]{:S(2)}, u32[]{:S(2)}) collective-permute-start(bf16[528,128]{1,0:T(8,128)(2,1)} %get-tuple-element.107), channel_id=1, source_target_pairs={{0,8},{4,12},{8,0},{12,4},{16,24},{20,28},{24,16},{28,20},{1,9},{5... | collective-permute-start | bytes 405512 | tf_op jit(solution)/shard_map/ppermute | solution.py:490
  78.7 5.9 %within1.1 = (f32[192,2048]{1,0:T(8,128)}, bf16[16,192,192]{2,1,0:T(8,128)(2,1)}) custom-call(s32[4]{0:T(128)} %pad_add_fusion.scal, f32[192,32]{1,0:T(8,128)} %get-tuple-element.63.cum.decay.refs_0_, f32[32,192]{1,0:T(8,128)} %get-tuple-element.64.flip.refs_1_, bf16[192,4096]{1,0:T(8,128)(2,1)} %refs_2_.9, bf16[192,4096]{1,0:T(8,128)(2,1)} %refs_1_.3, ...), custom_call_target="tpu_custom_call" | custom-call | flops 301989888 | bytes 4718592 | tf_op jit(solution)/shard_map/within1/pallas_call | solution.py:87
  84.6 0.6 copy-done.16
  85.3 7.6 %norm1.1 = (bf16[192,4096]{1,0:T(8,128)(2,1)}, bf16[192,2048]{1,0:T(8,128)(2,1)}, bf16[528,128]{1,0:T(8,128)(2,1)}, bf16[528,128]{1,0:T(8,128)(2,1)}, bf16[528,1...) custom-call(s32[4]{0:T(128)} %pad_add_fusion.scal, ...), custom_call_target="tpu_custom_call", output_to_operand_aliasing={{0}: (10, {})} | custom-call | flops 201326592 | bytes 4718592 | tf_op jit(solution)/shard_map/norm1/pallas_call | solution.py:87
  93.0 1.6 collective-permute-start.14
  94.5 2.0 %collective-permute-start.15 = (bf16[528,128]{1,0:T(8,128)(2,1)}, bf16[528,128]{1,0:T(8,128)(2,1)S(1)}, u32[]{:S(2)}, u32[]{:S(2)}) collective-permute-start(bf16[528,128]{1,0:T(8,128)(2,1)} %get-tuple-element.95), channel_id=1, source_target_pairs={{0,8},{4,12},{8,0},{12,4},{16,24},{20,28},{24,16},{28,20},{1,9},{5... | collective-permute-start | bytes 405512 | tf_op jit(solution)/shard_map/ppermute | solution.py:490
  96.5 0.6 copy-done.7
  97.2 0.1 copy-done.11
  97.3 2.8 %back_edge0.1 = (bf16[2,512,128]{2,1,0:T(8,128)(2,1)}, f32[8,128]{1,0:T(8,128)}) custom-call(s32[4]{0:T(128)} %pad_add_fusion.scal, bf16[528,128]{1,0:T(8,128)(2,1)} %get-tuple-element.105.refs_0_, bf16[528,128]{1,0:T(8,128)(2,1)} %copy-done.7, bf16[528,128]{1,0:T(8,128)(2,1)} %copy-done.9, bf16[528,128]{1,0:T(8,128)(2,1)} %copy-done.11, ...), custom_call_target="tpu_custom_call" | custom-call | flops 2621440 | bytes 786432 | tf_op jit(solution)/shard_map/back_edge0/pallas_call | solution.py:87
  100.1 1.3 collective-permute-start.25
  101.4 1.2 collective-permute-done.16.refs_3_
  102.6 0.6 copy-done.10
  103.3 2.8 %back_edge1.1 = (bf16[2,512,128]{2,1,0:T(8,128)(2,1)}, f32[8,128]{1,0:T(8,128)}) custom-call(s32[4]{0:T(128)} %pad_add_fusion.scal, bf16[528,128]{1,0:T(8,128)(2,1)} %get-tuple-element.93.refs_0_, bf16[528,128]{1,0:T(8,128)(2,1)} %copy-done.6, bf16[528,128]{1,0:T(8,128)(2,1)} %copy-done.8, bf16[528,128]{1,0:T(8,128)(2,1)} %copy-done.10, ...), custom_call_target="tpu_custom_call" | custom-call | flops 2621440 | bytes 786432 | tf_op jit(solution)/shard_map/back_edge1/pallas_call | solution.py:87
  106.1 1.5 collective-permute-start.17
  107.6 4.1 %collective-permute-start.26 = (f32[8,128]{1,0:T(8,128)}, f32[8,128]{1,0:T(8,128)S(1)}, u32[]{:S(2)}, u32[]{:S(2)}) collective-permute-start(f32[8,128]{1,0:T(8,128)} %get-tuple-element.110.refs_9_), channel_id=1, source_target_pairs={{0,16},{4,20},{8,24},{12,28},{16,0},{20,4},{24,8},{28,12},{1,17},{... | collective-permute-start | bytes 12296 | tf_op jit(solution)/shard_map/ppermute | solution.py:534
  111.7 13.6 %collective-permute-done.26.refs_10_ = f32[8,128]{1,0:T(8,128)S(1)} collective-permute-done((f32[8,128]{1,0:T(8,128)}, f32[8,128]{1,0:T(8,128)S(1)}, u32[]{:S(2)}, u32[]{:S(2)}) %collective-permute-start.26) | collective-permute-done | bytes 4128 | tf_op jit(solution)/shard_map/ppermute | solution.py:534
  125.3 0.6 copy-done.30
  125.8 0.7 copy-done.19
  126.5 3.1 %leave0.1 = (bf16[528,128]{1,0:T(8,128)(2,1)}, bf16[528,128]{1,0:T(8,128)(2,1)}, bf16[528,128]{1,0:T(8,128)(2,1)}, bf16[528,128]{1,0:T(8,128)(2,1)}) custom-call(s32[4]{0:T(128)} %pad_add_fusion.scal, bf16[528,128]{1,0:T(8,128)(2,1)} %get-tuple-element.105.refs_0_, bf16[528,128]{1,0:T(8,128)(2,1)} %copy-done.7, bf16[528,128]{1,0:T(8,128)(2,1)} %copy-done.9, ...), custom_call_target="tpu_custom_call" | custom-call | flops 3932160 | bytes 1310720 | tf_op jit(solution)/shard_map/leave0/pallas_call | solution.py:87
  129.7 1.5 collective-permute-start.27
  131.1 2.0 %collective-permute-start.29 = (bf16[528,128]{1,0:T(8,128)(2,1)}, bf16[528,128]{1,0:T(8,128)(2,1)S(1)}, u32[]{:S(2)}, u32[]{:S(2)}) collective-permute-start(bf16[528,128]{1,0:T(8,128)(2,1)} %get-tuple-element.114), channel_id=1, source_target_pairs={{0,12},{4,8},{8,4},{12,0},{16,28},{20,24},{24,20},{28,16},{1,13},{... | collective-permute-start | bytes 405512 | tf_op jit(solution)/shard_map/ppermute | solution.py:490
  133.1 2.8 %collective-permute-done.18.refs_10_ = f32[8,128]{1,0:T(8,128)S(1)} collective-permute-done((f32[8,128]{1,0:T(8,128)}, f32[8,128]{1,0:T(8,128)S(1)}, u32[]{:S(2)}, u32[]{:S(2)}) %collective-permute-start.18) | collective-permute-done | bytes 4128 | tf_op jit(solution)/shard_map/ppermute | solution.py:534
  136.0 0.6 copy-done.29
  136.5 0.7 copy-done.18
  137.2 3.2 %leave1.1 = (bf16[528,128]{1,0:T(8,128)(2,1)}, bf16[528,128]{1,0:T(8,128)(2,1)}, bf16[528,128]{1,0:T(8,128)(2,1)}, bf16[528,128]{1,0:T(8,128)(2,1)}) custom-call(s32[4]{0:T(128)} %pad_add_fusion.scal, bf16[528,128]{1,0:T(8,128)(2,1)} %get-tuple-element.93.refs_0_, bf16[528,128]{1,0:T(8,128)(2,1)} %copy-done.6, bf16[528,128]{1,0:T(8,128)(2,1)} %copy-done.8, ...), custom_call_target="tpu_custom_call" | custom-call | flops 3932160 | bytes 1310720 | tf_op jit(solution)/shard_map/leave1/pallas_call | solution.py:87
  140.4 0.5 collective-permute-start.19
  141.0 2.9 %collective-permute-start.21 = (bf16[528,128]{1,0:T(8,128)(2,1)}, bf16[528,128]{1,0:T(8,128)(2,1)S(1)}, u32[]{:S(2)}, u32[]{:S(2)}) collective-permute-start(bf16[528,128]{1,0:T(8,128)(2,1)} %get-tuple-element.102), channel_id=1, source_target_pairs={{0,12},{4,8},{8,4},{12,0},{16,28},{20,24},{24,20},{28,16},{1,13},{... | collective-permute-start | bytes 405512 | tf_op jit(solution)/shard_map/ppermute | solution.py:490
  143.9 9.0 %local0.1 = (bf16[192,4096]{1,0:T(8,128)(2,1)}, f32[192,2048]{1,0:T(8,128)}, f32[192,2048]{1,0:T(8,128)}) custom-call(s32[4]{0:T(128)} %pad_add_fusion.scal, f32[192,32]{1,0:T(8,128)} %get-tuple-element.63.cum.decay.refs_0_, f32[32,192]{1,0:T(8,128)} %get-tuple-element.64.flip.refs_1_, bf16[192,4096]{1,0:T(8,128)(2,1)} %refs_2_.9, ...), custom_call_target="tpu_custom_call" | custom-call | flops 754974720 | bytes 7864320 | tf_op jit(solution)/shard_map/local0/pallas_call | solution.py:87
  153.0 9.0 %local1.1 = (bf16[192,4096]{1,0:T(8,128)(2,1)}, f32[192,2048]{1,0:T(8,128)}, f32[192,2048]{1,0:T(8,128)}) custom-call(s32[4]{0:T(128)} %pad_add_fusion.scal, f32[192,32]{1,0:T(8,128)} %get-tuple-element.63.cum.decay.refs_0_, f32[32,192]{1,0:T(8,128)} %get-tuple-element.64.flip.refs_1_, bf16[192,4096]{1,0:T(8,128)(2,1)} %refs_2_.9, ...), custom_call_target="tpu_custom_call", output_to_operand_aliasing={{0}: (12, {})} | custom-call | flops 754974720 | bytes 7864320 | tf_op jit(solution)/shard_map/local1/pallas_call | solution.py:87
  162.0 0.6 copy-done.26
  162.7 5.8 %final0.1 = (bf16[192,4096]{1,0:T(8,128)(2,1)}, bf16[192,4096]{1,0:T(8,128)(2,1)}, f32[4,4,128]{2,1,0:T(4,128)}) custom-call(s32[4]{0:T(128)} %pad_add_fusion.scal, f32[192,32]{1,0:T(8,128)} %get-tuple-element.63.cum.decay.refs_0_, bf16[192,4096]{1,0:T(8,128)(2,1)} %refs_1_.3, bf16[192,4096]{1,0:T(8,128)(2,1)} %refs_2_.11, ...), custom_call_target="tpu_custom_call" | custom-call | flops 201326592 | bytes 6291456 | tf_op jit(solution)/shard_map/final0/pallas_call | solution.py:87
  168.5 0.6 copy-done.22
  169.2 0.1 copy-done.24
  169.3 5.9 %final1.1 = (bf16[192,4096]{1,0:T(8,128)(2,1)}, bf16[192,4096]{1,0:T(8,128)(2,1)}, f32[4,4,128]{2,1,0:T(4,128)}) custom-call(s32[4]{0:T(128)} %pad_add_fusion.scal, f32[192,32]{1,0:T(8,128)} %get-tuple-element.63.cum.decay.refs_0_, bf16[192,4096]{1,0:T(8,128)(2,1)} %refs_1_.3, ...), custom_call_target="tpu_custom_call", output_to_operand_aliasing={{0}: (10, {}), {1}: (11, {})} | custom-call | flops 201326592 | bytes 6291456 | tf_op jit(solution)/shard_map/final1/pallas_call | solution.py:87
  175.2 1.3 pad_maximum_fusion
  (83 shorter events, 0.6 us)
Async XLA Ops:
  9.5 13.1 %collective-permute-start.7 = (bf16[528,128]{1,0:T(8,128)(2,1)}, bf16[528,128]{1,0:T(8,128)(2,1)S(1)}, u32[]{:S(2)}, u32[]{:S(2)}) collective-permute-start(bf16[528,128]{1,0:T(8,128)(2,1)} %get-tuple-element.76), channel_id=1, source_target_pairs={{0,4},{4,0},{8,12},{12,8},{16,20},{20,16},{24,28},{28,24},{1,5},{5... | collective-permute-start | bytes 405512 | tf_op jit(solution)/shard_map/ppermute | solution.py:490
  12.6 10.1 %collective-permute-start.8 = (bf16[528,128]{1,0:T(8,128)(2,1)}, bf16[528,128]{1,0:T(8,128)(2,1)S(1)}, u32[]{:S(2)}, u32[]{:S(2)}) collective-permute-start(bf16[528,128]{1,0:T(8,128)(2,1)} %get-tuple-element.77), channel_id=1, source_target_pairs={{0,8},{4,12},{8,0},{12,4},{16,24},{20,28},{24,16},{28,20},{1,9},{5... | collective-permute-start | bytes 405512 | tf_op jit(solution)/shard_map/ppermute | solution.py:490
  14.1 8.6 %collective-permute-start.9 = (bf16[528,128]{1,0:T(8,128)(2,1)}, bf16[528,128]{1,0:T(8,128)(2,1)S(1)}, u32[]{:S(2)}, u32[]{:S(2)}) collective-permute-start(bf16[528,128]{1,0:T(8,128)(2,1)} %get-tuple-element.78), channel_id=1, source_target_pairs={{0,12},{4,8},{8,4},{12,0},{16,28},{20,24},{24,20},{28,16},{1,13},{... | collective-permute-start | bytes 405512 | tf_op jit(solution)/shard_map/ppermute | solution.py:490
  19.2 11.9 %collective-permute-start = (bf16[528,128]{1,0:T(8,128)(2,1)}, bf16[528,128]{1,0:T(8,128)(2,1)S(1)}, u32[]{:S(2)}, u32[]{:S(2)}) collective-permute-start(bf16[528,128]{1,0:T(8,128)(2,1)} %get-tuple-element.67), channel_id=1, source_target_pairs={{0,4},{4,0},{8,12},{12,8},{16,20},{20,16},{24,28},{28,24},{1,5},{5... | collective-permute-start | bytes 405512 | tf_op jit(solution)/shard_map/ppermute | solution.py:490
  21.1 10.1 %collective-permute-start.1 = (bf16[528,128]{1,0:T(8,128)(2,1)}, bf16[528,128]{1,0:T(8,128)(2,1)S(1)}, u32[]{:S(2)}, u32[]{:S(2)}) collective-permute-start(bf16[528,128]{1,0:T(8,128)(2,1)} %get-tuple-element.68), channel_id=1, source_target_pairs={{0,8},{4,12},{8,0},{12,4},{16,24},{20,28},{24,16},{28,20},{1,9},{5... | collective-permute-start | bytes 405512 | tf_op jit(solution)/shard_map/ppermute | solution.py:490
  22.7 0.7 copy-start.3
  22.7 8.5 %collective-permute-start.2 = (bf16[528,128]{1,0:T(8,128)(2,1)}, bf16[528,128]{1,0:T(8,128)(2,1)S(1)}, u32[]{:S(2)}, u32[]{:S(2)}) collective-permute-start(bf16[528,128]{1,0:T(8,128)(2,1)} %get-tuple-element.69), channel_id=1, source_target_pairs={{0,12},{4,8},{8,4},{12,0},{16,28},{20,24},{24,20},{28,16},{1,13},{... | collective-permute-start | bytes 405512 | tf_op jit(solution)/shard_map/ppermute | solution.py:490
  22.7 0.7 copy-start.4
  22.7 0.7 copy-start.5
  26.2 10.9 %collective-permute-start.10 = (bf16[2,512,128]{2,1,0:T(8,128)(2,1)}, bf16[2,512,128]{2,1,0:T(8,128)(2,1)S(1)}, u32[]{:S(2)}, u32[]{:S(2)}) collective-permute-start(bf16[2,512,128]{2,1,0:T(8,128)(2,1)} %edge0.1), channel_id=1, source_target_pairs={{0,16},{4,20},{8,24},{12,28},{1,17},{5,21},{9,25},{13,29},{2,18},{... | collective-permute-start | bytes 786440 | tf_op jit(solution)/shard_map/ppermute | solution.py:496
  31.1 0.6 copy-start
  31.1 0.7 copy-start.1
  31.2 0.7 copy-start.2
  34.7 18.7 %collective-permute-start.3 = (bf16[2,512,128]{2,1,0:T(8,128)(2,1)}, bf16[2,512,128]{2,1,0:T(8,128)(2,1)S(1)}, u32[]{:S(2)}, u32[]{:S(2)}) collective-permute-start(bf16[2,512,128]{2,1,0:T(8,128)(2,1)} %edge1.1), channel_id=1, source_target_pairs={{0,16},{4,20},{8,24},{12,28},{1,17},{5,21},{9,25},{13,29},{2,18},{... | collective-permute-start | bytes 786440 | tf_op jit(solution)/shard_map/ppermute | solution.py:496
  37.1 0.7 copy-start.21
  40.9 25.8 %collective-permute-start.11 = (bf16[512,128]{1,0:T(8,128)(2,1)}, bf16[512,128]{1,0:T(8,128)(2,1)S(1)}, u32[]{:S(2)}, u32[]{:S(2)}) collective-permute-start(bf16[512,128]{1,0:T(8,128)(2,1)} %get-tuple-element.80), channel_id=1, source_target_pairs={{0,4},{4,0},{8,12},{12,8},{16,20},{20,16},{24,28},{28,24},{1,5},{5... | collective-permute-start | bytes 393224 | tf_op jit(solution)/shard_map/ppermute | solution.py:490
  41.6 25.2 %collective-permute-start.12 = (bf16[512,128]{1,0:T(8,128)(2,1)}, bf16[512,128]{1,0:T(8,128)(2,1)S(1)}, u32[]{:S(2)}, u32[]{:S(2)}) collective-permute-start(bf16[512,128]{1,0:T(8,128)(2,1)} %get-tuple-element.81), channel_id=1, source_target_pairs={{0,8},{4,12},{8,0},{12,4},{16,24},{20,28},{24,16},{28,20},{1,9},{5... | collective-permute-start | bytes 393224 | tf_op jit(solution)/shard_map/ppermute | solution.py:490
  53.4 13.4 %collective-permute-start.13 = (bf16[512,128]{1,0:T(8,128)(2,1)}, bf16[512,128]{1,0:T(8,128)(2,1)S(1)}, u32[]{:S(2)}, u32[]{:S(2)}) collective-permute-start(bf16[512,128]{1,0:T(8,128)(2,1)} %get-tuple-element.82), channel_id=1, source_target_pairs={{0,12},{4,8},{8,4},{12,0},{16,28},{20,24},{24,20},{28,16},{1,13},{... | collective-permute-start | bytes 393224 | tf_op jit(solution)/shard_map/ppermute | solution.py:490
  53.4 0.7 copy-start.20
  57.1 21.5 %collective-permute-start.4 = (bf16[512,128]{1,0:T(8,128)(2,1)}, bf16[512,128]{1,0:T(8,128)(2,1)S(1)}, u32[]{:S(2)}, u32[]{:S(2)}) collective-permute-start(bf16[512,128]{1,0:T(8,128)(2,1)} %get-tuple-element.71), channel_id=1, source_target_pairs={{0,4},{4,0},{8,12},{12,8},{16,20},{20,16},{24,28},{28,24},{1,5},{5... | collective-permute-start | bytes 393224 | tf_op jit(solution)/shard_map/ppermute | solution.py:490
  58.6 6.0 %copy-start.32 = (bf16[512,128]{1,0:T(8,128)(2,1)S(1)}, bf16[512,128]{1,0:T(8,128)(2,1)}, u32[]{:S(2)}) copy-start(bf16[512,128]{1,0:T(8,128)(2,1)} %get-tuple-element.72) | copy-start | bytes 393220
  58.6 8.1 %copy-start.31 = (bf16[512,128]{1,0:T(8,128)(2,1)S(1)}, bf16[512,128]{1,0:T(8,128)(2,1)}, u32[]{:S(2)}) copy-start(bf16[512,128]{1,0:T(8,128)(2,1)} %get-tuple-element.73) | copy-start | bytes 393220
  64.6 20.0 %collective-permute-start.5 = (bf16[512,128]{1,0:T(8,128)(2,1)S(1)}, bf16[512,128]{1,0:T(8,128)(2,1)S(1)}, u32[]{:S(2)}, u32[]{:S(2)}) collective-permute-start(bf16[512,128]{1,0:T(8,128)(2,1)S(1)} %copy-done.32), channel_id=1, source_target_pairs={{0,8},{4,12},{8,0},{12,4},{16,24},{20,28},{24,16},{28,20},{1,9},{5... | collective-permute-start | bytes 393224 | tf_op jit(solution)/shard_map/ppermute | solution.py:490
  66.7 0.7 copy-start.12
  66.7 17.9 %collective-permute-start.6 = (bf16[512,128]{1,0:T(8,128)(2,1)S(1)}, bf16[512,128]{1,0:T(8,128)(2,1)S(1)}, u32[]{:S(2)}, u32[]{:S(2)}) collective-permute-start(bf16[512,128]{1,0:T(8,128)(2,1)S(1)} %copy-done.31), channel_id=1, source_target_pairs={{0,12},{4,8},{8,4},{12,0},{16,28},{20,24},{24,20},{28,16},{1,13},{... | collective-permute-start | bytes 393224 | tf_op jit(solution)/shard_map/ppermute | solution.py:490
  66.8 0.7 copy-start.13
  66.8 0.7 copy-start.14
  75.2 21.3 %collective-permute-start.22 = (bf16[528,128]{1,0:T(8,128)(2,1)}, bf16[528,128]{1,0:T(8,128)(2,1)S(1)}, u32[]{:S(2)}, u32[]{:S(2)}) collective-permute-start(bf16[528,128]{1,0:T(8,128)(2,1)} %get-tuple-element.106), channel_id=1, source_target_pairs={{0,4},{4,0},{8,12},{12,8},{16,20},{20,16},{24,28},{28,24},{1,5},{5... | collective-permute-start | bytes 405512 | tf_op jit(solution)/shard_map/ppermute | solution.py:490
  76.7 19.8 %collective-permute-start.23 = (bf16[528,128]{1,0:T(8,128)(2,1)}, bf16[528,128]{1,0:T(8,128)(2,1)S(1)}, u32[]{:S(2)}, u32[]{:S(2)}) collective-permute-start(bf16[528,128]{1,0:T(8,128)(2,1)} %get-tuple-element.107), channel_id=1, source_target_pairs={{0,8},{4,12},{8,0},{12,4},{16,24},{20,28},{24,16},{28,20},{1,9},{5... | collective-permute-start | bytes 405512 | tf_op jit(solution)/shard_map/ppermute | solution.py:490
  78.7 5.9 %copy-start.15 = (bf16[512,128]{1,0:T(8,128)(2,1)}, bf16[512,128]{1,0:T(8,128)(2,1)S(1)}, u32[]{:S(2)}) copy-start(bf16[512,128]{1,0:T(8,128)(2,1)S(1)} %collective-permute-done.4.refs_6_.refs_8_) | copy-start | bytes 393220
  78.7 17.8 %collective-permute-start.24 = (bf16[528,128]{1,0:T(8,128)(2,1)}, bf16[528,128]{1,0:T(8,128)(2,1)S(1)}, u32[]{:S(2)}, u32[]{:S(2)}) collective-permute-start(bf16[528,128]{1,0:T(8,128)(2,1)} %get-tuple-element.108), channel_id=1, source_target_pairs={{0,12},{4,8},{8,4},{12,0},{16,28},{20,24},{24,20},{28,16},{1,13},{... | collective-permute-start | bytes 405512 | tf_op jit(solution)/shard_map/ppermute | solution.py:490
  84.6 0.6 copy-start.16
  84.6 0.7 copy-start.17
  93.0 8.5 %collective-permute-start.14 = (bf16[528,128]{1,0:T(8,128)(2,1)}, bf16[528,128]{1,0:T(8,128)(2,1)S(1)}, u32[]{:S(2)}, u32[]{:S(2)}) collective-permute-start(bf16[528,128]{1,0:T(8,128)(2,1)} %get-tuple-element.94), channel_id=1, source_target_pairs={{0,4},{4,0},{8,12},{12,8},{16,20},{20,16},{24,28},{28,24},{1,5},{5... | collective-permute-start | bytes 405512 | tf_op jit(solution)/shard_map/ppermute | solution.py:490
  94.5 6.9 %collective-permute-start.15 = (bf16[528,128]{1,0:T(8,128)(2,1)}, bf16[528,128]{1,0:T(8,128)(2,1)S(1)}, u32[]{:S(2)}, u32[]{:S(2)}) collective-permute-start(bf16[528,128]{1,0:T(8,128)(2,1)} %get-tuple-element.95), channel_id=1, source_target_pairs={{0,8},{4,12},{8,0},{12,4},{16,24},{20,28},{24,16},{28,20},{1,9},{5... | collective-permute-start | bytes 405512 | tf_op jit(solution)/shard_map/ppermute | solution.py:490
  96.5 0.7 copy-start.7
  96.5 6.1 %collective-permute-start.16 = (bf16[528,128]{1,0:T(8,128)(2,1)}, bf16[528,128]{1,0:T(8,128)(2,1)S(1)}, u32[]{:S(2)}, u32[]{:S(2)}) collective-permute-start(bf16[528,128]{1,0:T(8,128)(2,1)} %get-tuple-element.96), channel_id=1, source_target_pairs={{0,12},{4,8},{8,4},{12,0},{16,28},{20,24},{24,20},{28,16},{1,13},{... | collective-permute-start | bytes 405512 | tf_op jit(solution)/shard_map/ppermute | solution.py:490
  96.5 0.7 copy-start.9
  96.5 0.7 copy-start.11
  100.1 25.1 %collective-permute-start.25 = (bf16[2,512,128]{2,1,0:T(8,128)(2,1)}, bf16[2,512,128]{2,1,0:T(8,128)(2,1)S(1)}, u32[]{:S(2)}, u32[]{:S(2)}) collective-permute-start(bf16[2,512,128]{2,1,0:T(8,128)(2,1)} %get-tuple-element.109), channel_id=1, source_target_pairs={{16,0},{20,4},{24,8},{28,12},{17,1},{21,5},{25,9},{29,13},{18,2},{... | collective-permute-start | bytes 786440 | tf_op jit(solution)/shard_map/ppermute | solution.py:496
  101.4 1.2 copy-start.6
  101.4 1.2 copy-start.8
  102.6 0.7 copy-start.10
  106.1 29.8 %collective-permute-start.17 = (bf16[2,512,128]{2,1,0:T(8,128)(2,1)}, bf16[2,512,128]{2,1,0:T(8,128)(2,1)S(1)}, u32[]{:S(2)}, u32[]{:S(2)}) collective-permute-start(bf16[2,512,128]{2,1,0:T(8,128)(2,1)} %get-tuple-element.97), channel_id=1, source_target_pairs={{16,0},{20,4},{24,8},{28,12},{17,1},{21,5},{25,9},{29,13},{18,2},{... | collective-permute-start | bytes 786440 | tf_op jit(solution)/shard_map/ppermute | solution.py:496
  107.6 17.7 %collective-permute-start.26 = (f32[8,128]{1,0:T(8,128)}, f32[8,128]{1,0:T(8,128)S(1)}, u32[]{:S(2)}, u32[]{:S(2)}) collective-permute-start(f32[8,128]{1,0:T(8,128)} %get-tuple-element.110.refs_9_), channel_id=1, source_target_pairs={{0,16},{4,20},{8,24},{12,28},{16,0},{20,4},{24,8},{28,12},{1,17},{... | collective-permute-start | bytes 12296 | tf_op jit(solution)/shard_map/ppermute | solution.py:534
  125.3 0.6 copy-start.30
  125.8 0.7 copy-start.19
  129.7 11.3 %collective-permute-start.27 = (bf16[528,128]{1,0:T(8,128)(2,1)}, bf16[528,128]{1,0:T(8,128)(2,1)S(1)}, u32[]{:S(2)}, u32[]{:S(2)}) collective-permute-start(bf16[528,128]{1,0:T(8,128)(2,1)} %get-tuple-element.112), channel_id=1, source_target_pairs={{0,4},{4,0},{8,12},{12,8},{16,20},{20,16},{24,28},{28,24},{1,5},{5... | collective-permute-start | bytes 405512 | tf_op jit(solution)/shard_map/ppermute | solution.py:490
  131.1 4.8 %collective-permute-start.18 = (f32[8,128]{1,0:T(8,128)}, f32[8,128]{1,0:T(8,128)S(1)}, u32[]{:S(2)}, u32[]{:S(2)}) collective-permute-start(f32[8,128]{1,0:T(8,128)} %get-tuple-element.98.refs_9_), channel_id=1, source_target_pairs={{0,16},{4,20},{8,24},{12,28},{16,0},{20,4},{24,8},{28,12},{1,17},{... | collective-permute-start | bytes 12296 | tf_op jit(solution)/shard_map/ppermute | solution.py:534
  131.1 30.8 %collective-permute-start.28 = (bf16[528,128]{1,0:T(8,128)(2,1)}, bf16[528,128]{1,0:T(8,128)(2,1)S(1)}, u32[]{:S(2)}, u32[]{:S(2)}) collective-permute-start(bf16[528,128]{1,0:T(8,128)(2,1)} %get-tuple-element.113), channel_id=1, source_target_pairs={{0,8},{4,12},{8,0},{12,4},{16,24},{20,28},{24,16},{28,20},{1,9},{5... | collective-permute-start | bytes 405512 | tf_op jit(solution)/shard_map/ppermute | solution.py:490
  131.1 30.8 %collective-permute-start.29 = (bf16[528,128]{1,0:T(8,128)(2,1)}, bf16[528,128]{1,0:T(8,128)(2,1)S(1)}, u32[]{:S(2)}, u32[]{:S(2)}) collective-permute-start(bf16[528,128]{1,0:T(8,128)(2,1)} %get-tuple-element.114), channel_id=1, source_target_pairs={{0,12},{4,8},{8,4},{12,0},{16,28},{20,24},{24,20},{28,16},{1,13},{... | collective-permute-start | bytes 405512 | tf_op jit(solution)/shard_map/ppermute | solution.py:490
  136.0 0.6 copy-start.29
  136.5 0.7 copy-start.18
  140.4 28.0 %collective-permute-start.19 = (bf16[528,128]{1,0:T(8,128)(2,1)}, bf16[528,128]{1,0:T(8,128)(2,1)S(1)}, u32[]{:S(2)}, u32[]{:S(2)}) collective-permute-start(bf16[528,128]{1,0:T(8,128)(2,1)} %get-tuple-element.100), channel_id=1, source_target_pairs={{0,4},{4,0},{8,12},{12,8},{16,20},{20,16},{24,28},{28,24},{1,5},{5... | collective-permute-start | bytes 405512 | tf_op jit(solution)/shard_map/ppermute | solution.py:490
  141.0 27.5 %collective-permute-start.20 = (bf16[528,128]{1,0:T(8,128)(2,1)}, bf16[528,128]{1,0:T(8,128)(2,1)S(1)}, u32[]{:S(2)}, u32[]{:S(2)}) collective-permute-start(bf16[528,128]{1,0:T(8,128)(2,1)} %get-tuple-element.101), channel_id=1, source_target_pairs={{0,8},{4,12},{8,0},{12,4},{16,24},{20,28},{24,16},{28,20},{1,9},{5... | collective-permute-start | bytes 405512 | tf_op jit(solution)/shard_map/ppermute | solution.py:490
  141.0 12.0 %copy-start.25 = (bf16[528,128]{1,0:T(8,128)(2,1)}, bf16[528,128]{1,0:T(8,128)(2,1)S(1)}, u32[]{:S(2)}) copy-start(bf16[528,128]{1,0:T(8,128)(2,1)S(1)} %collective-permute-done.27.refs_6_) | copy-start | bytes 405508
  141.0 27.5 %collective-permute-start.21 = (bf16[528,128]{1,0:T(8,128)(2,1)}, bf16[528,128]{1,0:T(8,128)(2,1)S(1)}, u32[]{:S(2)}, u32[]{:S(2)}) collective-permute-start(bf16[528,128]{1,0:T(8,128)(2,1)} %get-tuple-element.102), channel_id=1, source_target_pairs={{0,12},{4,8},{8,4},{12,0},{16,28},{20,24},{24,20},{28,16},{1,13},{... | collective-permute-start | bytes 405512 | tf_op jit(solution)/shard_map/ppermute | solution.py:490
  162.0 0.7 copy-start.26
  162.0 0.7 copy-start.27
  168.5 0.7 copy-start.22
  168.5 0.7 copy-start.23
  168.5 0.7 copy-start.24
  169.3 5.9 %copy-start.28 = (f32[4,4,128]{2,1,0:T(4,128)S(1)}, f32[4,4,128]{2,1,0:T(4,128)}, u32[]{:S(2)}) copy-start(f32[4,4,128]{2,1,0:T(4,128)} %get-tuple-element.119) | copy-start | bytes 24580
where the time goes:
time: 178 us; the launch traced here: 177 us
  Pallas kernels  91.2 us (51%)
  starting transfers between devices  52.4 us (29%)
  waiting for transfers between devices  17.6 us (10%)
  local copies, waits for them, and re-layouts  11.1 us (6%)
  between operations  2.33 us (1%)
  other arithmetic  1.91 us (1%)
    pallas_call x18, Pallas kernels, call(): pl.pallas_call(body, name=name, out_shape=outs, grid_spec=pltpu.PrefetchS...  91.2 us
    ppermute x24, starting transfers between devices, exchange(): out.append(lax.ppermute(pieces[k], 'seq', pairs))  38.3 us
    ppermute x2, waiting for transfers between devices, other_gain(): return lax.ppermute(gain, 'seq', [(i, i ^ GROUP) for i in range(p.devices)])  16.4 us
    unnamed x67, local copies, waits for them, and re-layouts  11.1 us
    ppermute x4, starting transfers between devices, shift(): return lax.ppermute(x, 'seq', pairs)  10 us
    ppermute x2, starting transfers between devices, other_gain(): return lax.ppermute(gain, 'seq', [(i, i ^ GROUP) for i in range(p.devices)])  4.09 us
  transfers between devices with their start and end apart: 30, of which 3 were waited for; matrix products, arithmetic and copies ran while one was open for 0% of the time, Pallas kernels for 45%

commit v1 on v0

v1 whole, which is shorter than its diff:
```python
import functools
import jax
import jax.numpy as jnp
from jax import lax
from jax.experimental import pallas as pl
from jax.experimental.pallas import tpu as pltpu
from jax.sharding import PartitionSpec as P

eps = 1e-06
highest = lax.Precision.HIGHEST
f32 = jnp.float32
bf16 = jnp.bfloat16
GROUP = 4
CHUNKS = 2
GRANT = 24 << 20


def dot(a, b, ca, cb):
    return lax.dot_general(a, b, (((ca,), (cb,)), ((), ())), preferred_element_type=f32)


def split3(x):
    hi = x.astype(bf16).astype(f32)
    mid = (x - hi).astype(bf16).astype(f32)
    low = (x - hi - mid).astype(bf16).astype(f32)
    return [hi, mid, low]


def pack_rows(rows, count):
    ids = lax.broadcasted_iota(jnp.int32, (count, rows[0].shape[-1]), 0)
    out = jnp.zeros(ids.shape, f32)
    for r, row in enumerate(rows):
        out = jnp.where(ids == r, row, out)
    return out.astype(bf16)


def column(cum, head):
    ids = lax.broadcasted_iota(jnp.int32, cum.shape, 1)
    return jnp.sum(jnp.where(ids == head, cum, 0.0), axis=1, keepdims=True)


class Plan:
    def __init__(self, length, heads, width, devices):
        self.length, self.heads, self.width, self.devices = length, heads, width, devices
        self.chunk_heads = heads // CHUNKS
        self.per = self.chunk_heads // GROUP
        self.rows = self.per * width
        self.extra = -(-(3 * self.per + 3) // 16) * 16
        self.piece = self.rows + self.extra
        self.tail = -(-3 * self.per * CHUNKS // 16) * 16
        self.cols = self.per * width
        self.chunk_cols = GROUP * self.cols

    def at(self, q, t):
        return pl.ds(pl.multiple_of(q * self.cols + t * self.width, self.width), self.width)

    def pieces_shape(self):
        return [jax.ShapeDtypeStruct((self.piece, self.width), bf16)] * GROUP


vmem = pl.BlockSpec(memory_space=pltpu.VMEM)
smem = pl.BlockSpec(memory_space=pltpu.SMEM)
hbm = pl.BlockSpec(memory_space=pltpu.HBM)


def outside(x):
    return pltpu.with_memory_space_constraint(x, pltpu.HBM)


anywhere = pl.BlockSpec(memory_space=pl.ANY)


def call(body, args, outs, out_specs, scratch, flops, moved, specs=None, aliases=None, after=None):
    args = list(args)
    specs = list(specs or [vmem] * len(args))
    skip = 0
    if after is not None:
        args.append(after)
        specs.append(anywhere)
        skip = 1
    count = len(args)

    def kernel(*refs):
        body(*refs[: count - skip], *refs[count:])

    return pl.pallas_call(
        kernel,
        out_shape=outs,
        in_specs=specs,
        out_specs=out_specs,
        scratch_shapes=scratch,
        input_output_aliases=aliases or {},
        compiler_params=pltpu.CompilerParams(vmem_limit_bytes=GRANT),
        cost_estimate=pl.CostEstimate(flops=flops, bytes_accessed=moved, transcendentals=0),
    )(*args)


def place():
    return lax.rem(lax.axis_index("seq"), GROUP)


def route(index, source, targets):
    for i, target in enumerate(targets):

        @pl.when(index == i)
        def _(target=target):
            target[...] = source[...]


def fetch(index, sources, target):
    for i, source in enumerate(sources):

        @pl.when(index == i)
        def _(source=source):
            target[...] = source[...]


def state_body(p, chunk, parent, fork, decay, keys, values, *refs):
    first = chunk == 0
    outs, refs = refs[:GROUP], refs[GROUP:]
    scaled_key, spread, refs = refs[0], refs[1], refs[2:]
    if first:
        flip, refs = refs[0], refs[1:]
    cum, blk, key_in, value_in, sems, small_sem, decay_in = refs
    if first:
        small = pltpu.make_async_copy(decay, decay_in, small_sem)
        small.start()
    for q in range(GROUP):
        cols = slice(q * p.cols, (q + 1) * p.cols)
        far = slice(chunk * p.chunk_cols + q * p.cols, chunk * p.chunk_cols + (q + 1) * p.cols)
        for j, (src, dst) in enumerate(((keys, key_in), (values, value_in))):
            pltpu.make_async_copy(src.at[:, far], dst.at[:, cols], sems.at[j, q]).start()
    if first:
        small.wait()
        rows = lax.broadcasted_iota(jnp.int32, (p.length, p.length), 0)
        cols = lax.broadcasted_iota(jnp.int32, (p.length, p.length), 1)
        tri = (rows <= cols).astype(f32)
        dims = (((1,), (0,)), ((), ()))
        flip[...] = lax.dot_general(decay_in[...], tri, dims, precision=highest, preferred_element_type=f32)
        cum[...] = jnp.transpose(flip[...])
    else:
        cum[...] = jnp.transpose(decay[...])
    me = place()
    position = lax.axis_index("seq")
    parent_id = parent[0]
    flags = [
        fork[0],
        (parent_id == position - 1).astype(jnp.int32),
        ((parent_id >= 0) & (parent_id != position - 1)).astype(jnp.int32),
    ]

    def group(q, _):
        for j, (src, dst) in enumerate(((keys, key_in), (values, value_in))):
            cols = pl.ds(pl.multiple_of(q * p.cols, p.cols), p.cols)
            pltpu.make_async_copy(src.at[:, cols], dst.at[:, cols], sems.at[j, q]).wait()
        marks = []
        for t in range(p.per):
            at = p.at(q, t)
            col = column(cum[...], chunk * p.chunk_heads + q * p.per + t)
            last = col[p.length - 1 : p.length]
            spread[:, at] = jnp.broadcast_to(col, (p.length, p.width))
            scaled = (key_in[:, at].astype(f32) * jnp.exp(last - col)).astype(bf16)
            scaled_key[:, at] = scaled
            blk[t * p.width : (t + 1) * p.width, :] = dot(scaled, value_in[:, at], 0, 0).astype(bf16)
            marks += split3(jnp.broadcast_to(jnp.exp(last), (1, p.width)))
        for flag in flags:
            marks.append(jnp.full((1, p.width), flag.astype(f32)))
        blk[p.rows :, :] = pack_rows(marks, p.extra)
        route(q ^ me, blk, outs)
        return 0

    lax.fori_loop(0, GROUP, group, 0)


def state_call(p, chunk, parent, fork, decay, keys, values, after=None):
    n = p.length
    outs = p.pieces_shape() + [
        jax.ShapeDtypeStruct((n, p.chunk_cols), bf16),
        jax.ShapeDtypeStruct((n, p.chunk_cols), f32),
    ]
    if chunk == 0:
        outs.append(jax.ShapeDtypeStruct((p.heads, n), f32))
    return call(
        functools.partial(state_body, p, chunk),
        (parent, fork, outside(decay) if chunk == 0 else decay, outside(keys), outside(values)),
        outs, [vmem] * len(outs),
        [
            pltpu.VMEM((n, p.heads), f32),
            pltpu.VMEM((p.piece, p.width), bf16),
            pltpu.VMEM((n, p.chunk_cols), bf16),
            pltpu.VMEM((n, p.chunk_cols), bf16),
            pltpu.SemaphoreType.DMA((2, GROUP)),
            pltpu.SemaphoreType.DMA,
            pltpu.VMEM((p.heads, n), f32),
        ],
        2 * n * p.width * p.chunk_cols, 4 * n * p.chunk_cols,
        [smem, smem, hbm if chunk == 0 else vmem, hbm, hbm], after=after,
    )


def within_body(p, chunk, flip, spread, queries, keys, values, within, weights, masks, scaled_query, scaled_value):
    n, w = p.length, p.width

    def group(q, _):
        for t in range(p.per):
            at = p.at(q, t)
            far = p.at(q + chunk * GROUP, t)
            index = q * p.per + t
            cols = spread[:, at]
            row = flip[pl.ds(chunk * p.chunk_heads + index, 1), :]
            rows_id = lax.broadcasted_iota(jnp.int32, (n, n), 0)
            cols_id = lax.broadcasted_iota(jnp.int32, (n, n), 1)
            diff = jnp.concatenate([cols, cols[:, : n - w]], axis=1) - row
            mask = jnp.exp(jnp.where(rows_id >= cols_id, diff, -jnp.inf))
            masks[index] = mask
            weighted = (dot(queries[:, far], keys[:, far], 1, 1) * mask).astype(bf16)
            weights[index] = weighted
            within[:, at] = dot(weighted, values[:, far], 1, 0)
            scaled_query[:, at] = (queries[:, far].astype(f32) * jnp.exp(cols)).astype(bf16)
            fall = jnp.exp(cols[n - 1 : n] - cols)
            scaled_value[:, at] = (values[:, far].astype(f32) * fall).astype(bf16)
        return 0

    lax.fori_loop(0, GROUP, group, 0)


def within_call(p, chunk, flip, spread, queries, keys, values, after=None):
    n, h = p.length, p.chunk_heads
    outs = [
        jax.ShapeDtypeStruct((n, p.chunk_cols), f32),
        jax.ShapeDtypeStruct((h, n, n), bf16),
        jax.ShapeDtypeStruct((h, n, n), f32),
        jax.ShapeDtypeStruct((n, p.chunk_cols), bf16),
        jax.ShapeDtypeStruct((n, p.chunk_cols), bf16),
    ]
    return call(
        functools.partial(within_body, p, chunk),
        (flip, spread, queries, keys, values), outs, [vmem] * len(outs), [],
        4 * n * n * p.chunk_cols, 12 * n * p.chunk_cols, after=after,
    )


def gather_pieces(refs, target):
    me = place()
    for k, ref in enumerate(refs):
        target[k ^ me] = ref[...]


def load_marks(p, marks, base, n, t):
    decay = sum(marks[n, base + 3 * t + j : base + 3 * t + j + 1, :].astype(f32) for j in range(3))
    at = base + 3 * p.per
    flag, alpha, beta = (marks[n, at + j : at + j + 1, :].astype(f32) > 0.5 for j in range(3))
    return decay, flag, alpha, beta


def forward_scan(p, start, scr, t, emit):
    branch, state = start
    at = slice(t * p.width, (t + 1) * p.width)
    for n in range(GROUP):
        decay, flag, alpha, beta = load_marks(p, scr, p.rows, n, t)
        entering = jnp.where(alpha, state, jnp.where(beta, branch, 0.0))
        if emit is not None:
            emit(n, at, entering)
            if n == GROUP - 1:
                break
        state = decay * entering + scr[n, at, :].astype(f32)
        branch = jnp.where(flag, state, branch)
    return branch, state


def backward_scan(p, start, scr, marks, t, emit):
    branch, state = start
    at = slice(t * p.width, (t + 1) * p.width)
    for n in reversed(range(GROUP)):
        decay, flag, alpha, beta = load_marks(p, marks, 0, n, t)
        leaving = jnp.where(flag, state + branch, state)
        if emit is not None:
            emit(n, at, leaving)
            if n == 0:
                break
        through = decay * leaving + scr[n, at, :].astype(f32)
        branch = jnp.where(flag, 0.0, branch) + jnp.where(beta, through, 0.0)
        state = jnp.where(alpha, through, 0.0)
    return branch, state


def zero_pair(p):
    zero = jnp.zeros((p.width, p.width), f32)
    return zero, zero


def edge_body(p, p0, p1, p2, p3, edge, scr):
    gather_pieces((p0, p1, p2, p3), scr)
    for t in range(p.per):
        branch, state = forward_scan(p, zero_pair(p), scr, t, None)
        edge[0, t * p.width : (t + 1) * p.width, :] = branch.astype(bf16)
        edge[1, t * p.width : (t + 1) * p.width, :] = state.astype(bf16)


def edge_call(p, pieces, after=None):
    return call(
        functools.partial(edge_body, p), pieces,
        jax.ShapeDtypeStruct((2, p.rows, p.width), bf16), vmem,
        [pltpu.VMEM((GROUP, p.piece, p.width), bf16)],
        40 * p.rows * p.width, 12 * p.rows * p.width, after=after,
    )


def enter_body(p, p0, p1, p2, p3, coming, o0, o1, o2, o3, scr, out):
    gather_pieces((p0, p1, p2, p3), scr)
    for t in range(p.per):
        at = slice(t * p.width, (t + 1) * p.width)
        start = (coming[0, at, :].astype(f32), coming[1, at, :].astype(f32))

        def emit(n, at, value):
            out[n, at, :] = value.astype(bf16)

        forward_scan(p, start, scr, t, emit)
    me = place()
    for k, ref in enumerate((o0, o1, o2, o3)):
        ref[...] = out[k ^ me]


def enter_call(p, pieces, coming, after=None):
    return call(
        functools.partial(enter_body, p), (*pieces, coming),
        [jax.ShapeDtypeStruct((p.rows, p.width), bf16)] * GROUP, [vmem] * GROUP,
        [pltpu.VMEM((GROUP, p.piece, p.width), bf16), pltpu.VMEM((GROUP, p.rows, p.width), bf16)],
        60 * p.rows * p.width, 20 * p.rows * p.width, after=after,
    )


def send_out(p, chunk, q, source, target, sem):
    cols = pl.ds(pl.multiple_of(q * p.cols, p.cols), p.cols)
    far = pl.ds(pl.multiple_of(chunk * p.chunk_cols + q * p.cols, p.cols), p.cols)
    return pltpu.make_async_copy(source.at[:, cols], target.at[:, far], sem.at[q])


def norm_body(p, chunk, within, scaled_query, grads, gain, *refs):
    states, refs = refs[:GROUP], refs[GROUP + (chunk > 0) :]
    attended, grad_b = refs[0], refs[1]
    outs, (blk, state, buf, sem) = refs[2 : 2 + GROUP], refs[2 + GROUP :]
    me = place()

    def group(q, _):
        fetch(q ^ me, states, state)
        marks = []
        for t in range(p.per):
            at, far = p.at(q, t), p.at(q + chunk * GROUP, t)
            rows = slice(t * p.width, (t + 1) * p.width)
            scaled = scaled_query[:, at]
            attention = within[:, at] + dot(scaled, state[rows, :], 1, 0)
            scale = lax.rsqrt(jnp.mean(attention * attention, axis=-1, keepdims=True) + eps)
            normed = attention * scale
            gain_row = gain[:, far]
            buf[:, at] = (normed * gain_row).astype(bf16)
            lean = grads[:, far].astype(f32) * normed
            pull = jnp.mean(lean * gain_row, axis=-1, keepdims=True)
            grad = ((grads[:, far].astype(f32) * gain_row - normed * pull) * scale).astype(bf16)
            grad_b[:, at] = grad
            blk[rows, :] = dot(scaled, grad, 0, 0).astype(bf16)
            marks += split3(jnp.sum(lean, axis=0, keepdims=True))
        blk[p.rows :, :] = pack_rows(marks, p.extra)
        route(q ^ me, blk, outs)
        send_out(p, chunk, q, buf, attended, sem).start()
        return 0

    lax.fori_loop(0, GROUP, group, 0)
    for q in range(GROUP):
        send_out(p, chunk, q, buf, attended, sem).wait()


def norm_call(p, chunk, within, scaled_query, grads, gain, states, attended, after=None):
    n = p.length
    args = [within, scaled_query, grads, gain, *states]
    specs = [vmem] * len(args)
    aliases = None
    if chunk > 0:
        aliases = {len(args): 0}
        args.append(attended)
        specs.append(hbm)
    full = jax.ShapeDtypeStruct((n, p.heads * p.width), bf16)
    return call(
        functools.partial(norm_body, p, chunk), args,
        [full, jax.ShapeDtypeStruct((n, p.chunk_cols), bf16)] + p.pieces_shape(),
        [hbm, vmem] + [vmem] * GROUP,
        [
            pltpu.VMEM((p.piece, p.width), bf16),
            pltpu.VMEM((p.rows, p.width), bf16),
            pltpu.VMEM((n, p.chunk_cols), bf16),
            pltpu.SemaphoreType.DMA((GROUP,)),
        ],
        4 * n * p.width * p.chunk_cols, 12 * n * p.chunk_cols, specs, aliases, after,
    )


def local_body(p, chunk, spread, masks, queries, keys, values, grad_b, weights, *refs):
    states, refs = refs[:GROUP], refs[GROUP + (chunk > 0) :]
    query_grad, key_local, value_local, state, buf, sem = refs
    me = place()

    def group(q, _):
        fetch(q ^ me, states, state)
        for t in range(p.per):
            at, far = p.at(q, t), p.at(q + chunk * GROUP, t)
            rows = slice(t * p.width, (t + 1) * p.width)
            index = q * p.per + t
            grad = grad_b[:, at]
            grad_weights = (dot(grad, values[:, far], 1, 1) * masks[index]).astype(bf16)
            across = jnp.exp(spread[:, at]) * dot(grad, state[rows, :], 1, 1)
            buf[:, at] = (dot(grad_weights, keys[:, far], 1, 0) + across).astype(bf16)
            key_local[:, at] = dot(grad_weights, queries[:, far], 0, 0)
            value_local[:, at] = dot(weights[index], grad, 0, 0)
        send_out(p, chunk, q, buf, query_grad, sem).start()
        return 0

    lax.fori_loop(0, GROUP, group, 0)
    for q in range(GROUP):
        send_out(p, chunk, q, buf, query_grad, sem).wait()


def local_call(p, chunk, spread, masks, queries, keys, values, grad_b, weights, states, query_grad, after=None):
    n = p.length
    args = [spread, masks, queries, keys, values, grad_b, weights, *states]
    specs = [vmem] * len(args)
    aliases = None
    if chunk > 0:
        aliases = {len(args): 0}
        args.append(query_grad)
        specs.append(hbm)
    return call(
        functools.partial(local_body, p, chunk), args,
        [jax.ShapeDtypeStruct((n, p.heads * p.width), bf16)]
        + [jax.ShapeDtypeStruct((n, p.chunk_cols), f32)] * 2,
        [hbm, vmem, vmem],
        [
            pltpu.VMEM((p.rows, p.width), bf16),
            pltpu.VMEM((n, p.chunk_cols), bf16),
            pltpu.SemaphoreType.DMA((GROUP,)),
        ],
        10 * n * n * p.chunk_cols, 20 * n * p.chunk_cols, specs, aliases, after,
    )


def back_edge_body(p, chunk, *refs):
    pulls, pieces, refs = refs[:GROUP], refs[GROUP : 2 * GROUP], refs[2 * GROUP :]
    edge, gain_sum, scr, marks = refs[chunk > 0 :]
    gather_pieces(pulls, scr)
    gather_marks(p, pieces, marks)
    for t in range(p.per):
        branch, state = backward_scan(p, zero_pair(p), scr, marks, t, None)
        edge[0, t * p.width : (t + 1) * p.width, :] = branch.astype(bf16)
        edge[1, t * p.width : (t + 1) * p.width, :] = state.astype(bf16)
    gain = refs[0][...] if chunk > 0 else jnp.zeros(gain_sum.shape, f32)
    ids = lax.broadcasted_iota(jnp.int32, gain.shape, 0)
    for t in range(p.per):
        row = 0.0
        for n in range(GROUP):
            for j in range(3):
                at = p.rows + 3 * t + j
                row = row + scr[n, at : at + 1, :].astype(f32)
        gain = jnp.where(ids == chunk * p.per + t, row, gain)
    gain_sum[...] = gain


def gather_marks(p, refs, target):
    me = place()
    for k, ref in enumerate(refs):
        target[k ^ me] = ref[p.rows :, :]


def back_edge_call(p, chunk, pulls, pieces, gain_sum, after=None):
    wide = -(-p.per * CHUNKS // 8) * 8
    before = (gain_sum,) if chunk > 0 else ()
    return call(
        functools.partial(back_edge_body, p, chunk), (*pulls, *pieces, *before),
        [jax.ShapeDtypeStruct((2, p.rows, p.width), bf16), jax.ShapeDtypeStruct((wide, p.width), f32)],
        [vmem, vmem],
        [pltpu.VMEM((GROUP, p.piece, p.width), bf16), pltpu.VMEM((GROUP, p.extra, p.width), bf16)],
        40 * p.rows * p.width, 12 * p.rows * p.width, after=after,
    )


def leave_body(p, first, *refs):
    pulls, pieces, refs = refs[:GROUP], refs[GROUP : 2 * GROUP], refs[2 * GROUP :]
    coming, refs = refs[0], refs[1:]
    if first:
        gain_sum, *refs = refs
    outs, (scr, marks, out) = refs[:GROUP], refs[GROUP:]
    gather_pieces(pulls, scr)
    gather_marks(p, pieces, marks)
    for t in range(p.per):
        at = slice(t * p.width, (t + 1) * p.width)
        start = (coming[0, at, :].astype(f32), coming[1, at, :].astype(f32))

        def emit(n, at, value):
            out[n, at, :] = value.astype(bf16)

        backward_scan(p, start, scr, marks, t, emit)
    if first:
        rows = []
        for t in range(p.per * CHUNKS):
            rows += split3(gain_sum[t : t + 1, :])
        tail = pack_rows(rows, p.tail)
    me = place()
    for k, ref in enumerate(outs):
        ref[: p.rows, :] = out[k ^ me]
        if first:
            ref[p.rows :, :] = tail


def leave_call(p, chunk, pulls, pieces, coming, gains, after=None):
    first = chunk == 0
    height = p.rows + (p.tail if first else 0)
    return call(
        functools.partial(leave_body, p, first),
        (*pulls, *pieces, coming, *gains),
        [jax.ShapeDtypeStruct((height, p.width), bf16)] * GROUP, [vmem] * GROUP,
        [
            pltpu.VMEM((GROUP, p.piece, p.width), bf16),
            pltpu.VMEM((GROUP, p.extra, p.width), bf16),
            pltpu.VMEM((GROUP, p.rows, p.width), bf16),
        ],
        60 * p.rows * p.width, 20 * p.rows * p.width, after=after,
    )


def final_body(p, chunk, scaled_key, scaled_value, key_local, value_local, *refs):
    first = chunk == 0
    states, refs = refs[:GROUP], refs[GROUP:]
    if not first:
        gain_mine, gain_other, refs = refs[0], refs[1], refs[4:]
    key_grad, value_grad, gain_out, state, key_buf, value_buf, sem, *more = refs
    me = place()

    def group(q, _):
        fetch(q ^ me, states, state)
        for t in range(p.per):
            at = p.at(q, t)
            rows = slice(t * p.width, (t + 1) * p.width)
            key_buf[:, at] = (key_local[:, at] + dot(scaled_value[:, at], state[rows, :], 1, 1)).astype(bf16)
            value_buf[:, at] = (value_local[:, at] + dot(scaled_key[:, at], state[rows, :], 1, 0)).astype(bf16)
        if first:
            more[0][q] = state[p.rows :, :].astype(f32)
        send_out(p, chunk, q, key_buf, key_grad, sem.at[0]).start()
        send_out(p, chunk, q, value_buf, value_grad, sem.at[1]).start()
        return 0

    lax.fori_loop(0, GROUP, group, 0)
    if first:
        total = jnp.zeros(gain_out.shape, f32)
        ids = lax.broadcasted_iota(jnp.int32, total.shape, 0)
        for h in range(p.heads):
            c, q, t = h // p.chunk_heads, h % p.chunk_heads // p.per, h % p.per
            base = 3 * (c * p.per + t)
            row = sum(more[0][q, base + j : base + j + 1, :] for j in range(3))
            total = jnp.where(ids == h, row, total)
        gain_out[...] = total
    elif chunk == CHUNKS - 1:
        gain_out[...] = gain_mine[...] + gain_other[...]
    else:
        gain_out[...] = gain_mine[...]
    for q in range(GROUP):
        send_out(p, chunk, q, key_buf, key_grad, sem.at[0]).wait()
        send_out(p, chunk, q, value_buf, value_grad, sem.at[1]).wait()


def final_call(p, chunk, scaled_key, scaled_value, key_local, value_local, states, gains, key_grad, value_grad, after=None):
    n = p.length
    first = chunk == 0
    args = [scaled_key, scaled_value, key_local, value_local, *states]
    specs = [vmem] * len(args)
    aliases = None
    if not first:
        aliases = {len(args) + 2: 0, len(args) + 3: 1}
        args += [*gains, key_grad, value_grad]
        specs += [vmem, vmem, hbm, hbm]
    full = jax.ShapeDtypeStruct((n, p.heads * p.width), bf16)
    scratch = [
        pltpu.VMEM(states[0].shape, bf16),
        pltpu.VMEM((n, p.chunk_cols), bf16),
        pltpu.VMEM((n, p.chunk_cols), bf16),
        pltpu.SemaphoreType.DMA((2, GROUP)),
    ]
    if first:
        scratch.append(pltpu.VMEM((GROUP, p.tail, p.width), f32))
    return call(
        functools.partial(final_body, p, chunk), args,
        [full, full, jax.ShapeDtypeStruct((p.heads, p.width), f32)],
        [hbm, hbm, vmem],
        scratch,
        4 * n * p.width * p.chunk_cols, 16 * n * p.chunk_cols, specs, aliases, after,
    )


def exchange(p, pieces):
    out = [pieces[0]]
    for k in range(1, GROUP):
        pairs = [(i, i ^ k) for i in range(p.devices)]
        out.append(lax.ppermute(pieces[k], "seq", pairs))
    return out


def shift(p, x, groups):
    pairs = [(i, i + GROUP * groups) for i in range(p.devices) if 0 <= i + GROUP * groups < p.devices]
    return lax.ppermute(x, "seq", pairs)


def group_matrix(p, pieces):
    marks = jnp.stack([piece[p.rows :, 0] for piece in pieces]).astype(f32)
    marks = marks[jnp.arange(GROUP) ^ place()]
    at = 3 * p.per
    decay = marks[:, :at].reshape(GROUP, p.per, 3).sum(-1)
    flag, alpha, beta = (marks[:, at + j : at + j + 1] for j in range(3))
    top = jnp.stack([1.0 - flag + flag * decay * beta, flag * decay * alpha], axis=-1)
    low = jnp.stack([decay * beta, decay * alpha], axis=-1)
    coef = jnp.stack([top, low], axis=2)
    total = coef[0]
    for n in range(1, GROUP):
        total = jnp.einsum("hab,hbc->hac", coef[n], total, precision=highest)
    return total


def across(p, edge, matrix, sign):
    groups = p.devices // GROUP
    if groups <= 2:
        return shift(p, edge, sign)
    shape = (2, p.per, p.width, p.width)
    carry = shift(p, edge, sign).astype(f32).reshape(shape)
    moved = shift(p, matrix, sign)
    reach = 1
    while reach < groups - 1:
        carry_far = shift(p, carry, sign * reach)
        moved_far = shift(p, moved, sign * reach)
        carry = carry + jnp.einsum("hab,bhxy->ahxy", moved, carry_far, precision=highest)
        moved = jnp.einsum("hab,hbc->hac", moved, moved_far, precision=highest)
        reach *= 2
    return carry.astype(bf16).reshape(edge.shape)


def other_gain(p, gain):
    groups = p.devices // GROUP
    if groups == 2:
        return lax.ppermute(gain, "seq", [(i, i ^ GROUP) for i in range(p.devices)])
    same = [[g * GROUP + q for g in range(groups)] for q in range(GROUP)]
    return lax.psum(gain, "seq", axis_index_groups=same) - gain


ORDER = (
    "state0",
    "state1",
    "within0",
    "edge0",
    "within1",
    "edge1",
    "enter0",
    "norm0",
    "enter1",
    "back_edge0",
    "norm1",
    "local0",
    "back_edge1",
    "leave0",
    "local1",
    "final0",
    "leave1",
    "final1",
)


def on_device(
    queries, key_vectors, value_vectors, output_grad, log_decay, norm_gain, parent, fork_flag
):
    length, heads = log_decay.shape
    width = queries.shape[1] // heads
    p = Plan(length, heads, width, lax.axis_size("seq"))
    many = p.devices // GROUP > 2
    gain = norm_gain.reshape(1, heads * width)
    v = {}
    last = None

    def chained(make, pick):
        nonlocal last
        out = make(last)
        last = pick(out)
        return out

    flip = jnp.transpose(log_decay)
    attended = query_grad = key_grad = value_grad = total_gain = gain_sum = None
    for step in ORDER:
        kind, c = step[:-1], int(step[-1])
        if kind == "state":
            out = chained(
                lambda a: state_call(p, c, parent, fork_flag, flip, key_vectors, value_vectors, a),
                lambda o: o[GROUP + 1],
            )
            v["scaled_key", c], v["spread", c] = out[GROUP], out[GROUP + 1]
            if c == 0:
                flip = out[GROUP + 2]
            v["pieces", c] = exchange(p, out[:GROUP])
        elif kind == "within":
            out = chained(
                lambda a: within_call(p, c, flip, v["spread", c], queries, key_vectors, value_vectors, a),
                lambda o: o[0],
            )
            v["within", c], v["weights", c], v["masks", c], v["scaled_query", c], v["scaled_value", c] = out
        elif kind == "edge":
            pieces = v["pieces", c]
            v["matrix", c] = group_matrix(p, pieces) if many else None
            edge = chained(lambda a: edge_call(p, pieces, a), lambda o: o)
            v["coming", c] = across(p, edge, v["matrix", c], 1)
        elif kind == "enter":
            out = chained(lambda a: enter_call(p, v["pieces", c], v["coming", c], a), lambda o: o[0])
            v["states", c] = exchange(p, out)
        elif kind == "norm":
            out = chained(
                lambda a: norm_call(
                    p, c, v["within", c], v["scaled_query", c], output_grad, gain, v["states", c], attended, a
                ),
                lambda o: o[1],
            )
            attended, v["grad", c] = out[0], out[1]
            v["pulls", c] = exchange(p, out[2:])
        elif kind == "local":
            query_grad, v["key", c], v["value", c] = chained(
                lambda a: local_call(
                    p, c, v["spread", c], v["masks", c], queries, key_vectors, value_vectors,
                    v["grad", c], v["weights", c], v["states", c], query_grad, a,
                ),
                lambda o: o[1],
            )
        elif kind == "back_edge":
            edge, v["gain", c] = chained(
                lambda a: back_edge_call(p, c, v["pulls", c], v["pieces", c], gain_sum, a), lambda o: o[1]
            )
            flipped = jnp.swapaxes(v["matrix", c], 1, 2) if many else None
            v["back", c] = across(p, edge, flipped, -1)
            gain_sum = v["gain", c]
        elif kind == "leave":
            gains = (gain_sum,) if c == 0 else ()
            out = chained(
                lambda a: leave_call(p, c, v["pulls", c], v["pieces", c], v["back", c], gains, a),
                lambda o: o[0],
            )
            v["grads", c] = exchange(p, out)
        else:
            gains = (total_gain, total_gain)
            if c == CHUNKS - 1:
                gains = (total_gain, other_gain(p, total_gain))
            key_grad, value_grad, total_gain = chained(
                lambda a: final_call(
                    p, c, v["scaled_key", c], v["scaled_value", c], v["key", c], v["value", c],
                    v["grads", c], gains, key_grad, value_grad, a,
                ),
                lambda o: o[2],
            )
    return attended, query_grad, key_grad, value_grad, total_gain.reshape(-1)


def solution(mesh):
    rows = P(("leaf", "seq"), None)
    flat = P(("leaf", "seq"))
    return jax.shard_map(
        on_device,
        mesh=mesh,
        in_specs=(rows, rows, rows, rows, rows, P(), flat, flat),
        out_specs=(rows, rows, rows, rows, P("leaf")),
        check_vma=False,
    )
```

time: 178 us -> 108 us (0.61)
  Pallas kernels: 91.2 us -> 40.7 us
  local copies, waits for them, and re-layouts: 11.1 us -> 0.02 us
  starting transfers between devices: 52.4 us -> 42.8 us
  waiting for transfers between devices: 17.6 us -> 21.6 us
  other arithmetic: 1.91 us -> 0 us
    pallas_call x18, Pallas kernels: 91.2 us -> 40.7 us  [call(): pl.pallas_call(kernel, out_shape=outs, in_specs=specs, out_specs=out_spec...]
    ppermute x24, waiting for transfers between devices: 1.23 us -> 18.5 us  [exchange(): out.append(lax.ppermute(pieces[k], 'seq', pairs))]
    ppermute x2 -> x1, waiting for transfers between devices: 16.4 us -> 3.08 us  [other_gain(): return lax.ppermute(gain, 'seq', [(i, i ^ GROUP) for i in range(p.devices)])]
    unnamed x67 -> x10, local copies, waits for them, and re-layouts: 11.1 us -> 0.02 us
    ppermute x24, starting transfers between devices: 38.3 us -> 31.1 us  [exchange(): out.append(lax.ppermute(pieces[k], 'seq', pairs))]
    ppermute x2 -> x1, starting transfers between devices: 4.09 us -> 1.56 us  [other_gain(): return lax.ppermute(gain, 'seq', [(i, i ^ GROUP) for i in range(p.devices)])]
  transfers between devices with their start and end apart: 30 -> 29, of which waited for: 3 -> 10; matrix products, arithmetic and copies ran while one was open for 0% -> 0% of each run, Pallas kernels for 45% -> 31%
where the time goes in v1:
time: 108 us; the launch traced here: 107 us
  starting transfers between devices  42.8 us (40%)
  Pallas kernels  40.7 us (38%)
  waiting for transfers between devices  21.6 us (20%)
  between operations  2.23 us (2%)
    pallas_call x18, Pallas kernels, call(): pl.pallas_call(kernel, out_shape=outs, in_specs=specs, out_specs=out_spec...  40.7 us
    ppermute x24, starting transfers between devices, exchange(): out.append(lax.ppermute(pieces[k], 'seq', pairs))  31.1 us
    ppermute x24, waiting for transfers between devices, exchange(): out.append(lax.ppermute(pieces[k], 'seq', pairs))  18.5 us
    ppermute x4, starting transfers between devices, shift(): return lax.ppermute(x, 'seq', pairs)  10.2 us
    ppermute x1, waiting for transfers between devices, other_gain(): return lax.ppermute(gain, 'seq', [(i, i ^ GROUP) for i in range(p.devices)])  3.08 us
  transfers between devices with their start and end apart: 29, of which 10 were waited for; matrix products, arithmetic and copies ran while one was open for 0% of the time, Pallas kernels for 31%

profile of v1, /device:TPU:0, one launch (start us, length us, event | category | flops | bytes accessed | tf_op | source)
XLA Modules:
  0.0 107.4 jit_solution(7502904292259340734)
XLA Ops:
  1.9 3.6 %shard_map.119 = (bf16[528,128]{1,0:T(8,128)(2,1)S(1)}, bf16[528,128]{1,0:T(8,128)(2,1)S(1)}, bf16[528,128]{1,0:T(8,128)(2,1)S(1)}, bf16[528,128]{1,0:T(8,128)(2...) custom-call(s32[1]{0:T(128)S(6)} %copy.21.refs_0_, s32[1]{0:T(128)S(6)} %copy.22.refs_1_, ...), custom_call_target="tpu_custom_call" | custom-call | flops 100663296 | bytes 1572864 | tf_op jit(solution)/shard_map/pallas_call | solution.py:86
  5.5 3.1 %collective-permute-start = (bf16[528,128]{1,0:T(8,128)(2,1)S(1)}, bf16[528,128]{1,0:T(8,128)(2,1)S(1)}, u32[]{:S(2)}, u32[]{:S(2)}) collective-permute-start(bf16[528,128]{1,0:T(8,128)(2,1)S(1)} %get-tuple-element.76), channel_id=1, source_target_pairs={{0,4},{4,0},{8,12},{12,8},{16,20},{20,16},{24,28},{28,24},{1,5},{5... | collective-permute-start | bytes 405512 | tf_op jit(solution)/shard_map/ppermute | solution.py:600
  8.6 1.6 %collective-permute-start.1 = (bf16[528,128]{1,0:T(8,128)(2,1)S(1)}, bf16[528,128]{1,0:T(8,128)(2,1)S(1)}, u32[]{:S(2)}, u32[]{:S(2)}) collective-permute-start(bf16[528,128]{1,0:T(8,128)(2,1)S(1)} %get-tuple-element.77), channel_id=1, source_target_pairs={{0,8},{4,12},{8,0},{12,4},{16,24},{20,28},{24,16},{28,20},{1,9},{5... | collective-permute-start | bytes 405512 | tf_op jit(solution)/shard_map/ppermute | solution.py:600
  10.2 0.0 collective-permute-start.2
  10.2 3.2 %shard_map.120 = (bf16[528,128]{1,0:T(8,128)(2,1)S(1)}, bf16[528,128]{1,0:T(8,128)(2,1)S(1)}, bf16[528,128]{1,0:T(8,128)(2,1)S(1)}, bf16[528,128]{1,0:T(8,128)(2...) custom-call(s32[1]{0:T(128)S(6)} %copy.21.refs_0_, s32[1]{0:T(128)S(6)} %copy.22.refs_1_, ...), custom_call_target="tpu_custom_call" | custom-call | flops 100663296 | bytes 1572864 | tf_op jit(solution)/shard_map/pallas_call | solution.py:86
  13.4 2.5 %shard_map.121 = (f32[192,2048]{1,0:T(8,128)S(1)}, bf16[16,192,192]{2,1,0:T(8,128)(2,1)S(1)}, f32[16,192,192]{2,1,0:T(8,128)S(1)}, bf16[192,2048]{1,0:T(8,128)(2,1)S(1)}, bf16[192,2048]{1,0:T(8,128)(2,1)S(1)}) custom-call(f32[32,192]{1,0:T(8,128)S(1)} %get-tuple-element.72.refs_2_.refs_0_, f32[192,2048]{1,0:T(8,128)S(1)} %get-tuple-element.73.refs_5_.refs_1_.refs_0_, ...), custom_call_target="tpu_custom_call" | custom-call | flops 301989888 | bytes 4718592 | tf_op jit(solution)/shard_map/pallas_call | solution.py:86
  15.9 0.0 collective-permute-done.1.refs_2_.refs_6_
  15.9 0.4 collective-permute-done.2.refs_3_.refs_7_
  16.3 0.3 shard_map.122.refs_5_
  16.6 4.7 %collective-permute-start.7 = (bf16[2,512,128]{2,1,0:T(8,128)(2,1)S(1)}, bf16[2,512,128]{2,1,0:T(8,128)(2,1)S(1)}, u32[]{:S(2)}, u32[]{:S(2)}) collective-permute-start(bf16[2,512,128]{2,1,0:T(8,128)(2,1)S(1)} %shard_map.122.refs_5_), channel_id=1, source_target_pairs={{0,16},{4,20},{8,24},{12,28},{1,17},{5,21},{9,25},{13,29},{2,18},{... | collective-permute-start | bytes 786440 | tf_op jit(solution)/shard_map/ppermute | solution.py:606
  21.3 1.6 %collective-permute-start.3 = (bf16[528,128]{1,0:T(8,128)(2,1)S(1)}, bf16[528,128]{1,0:T(8,128)(2,1)S(1)}, u32[]{:S(2)}, u32[]{:S(2)}) collective-permute-start(bf16[528,128]{1,0:T(8,128)(2,1)S(1)} %get-tuple-element.83), channel_id=1, source_target_pairs={{0,4},{4,0},{8,12},{12,8},{16,20},{20,16},{24,28},{28,24},{1,5},{5... | collective-permute-start | bytes 405512 | tf_op jit(solution)/shard_map/ppermute | solution.py:600
  22.8 1.6 %collective-permute-start.4 = (bf16[528,128]{1,0:T(8,128)(2,1)S(1)}, bf16[528,128]{1,0:T(8,128)(2,1)S(1)}, u32[]{:S(2)}, u32[]{:S(2)}) collective-permute-start(bf16[528,128]{1,0:T(8,128)(2,1)S(1)} %get-tuple-element.84), channel_id=1, source_target_pairs={{0,8},{4,12},{8,0},{12,4},{16,24},{20,28},{24,16},{28,20},{1,9},{5... | collective-permute-start | bytes 405512 | tf_op jit(solution)/shard_map/ppermute | solution.py:600
  24.4 0.4 collective-permute-start.5
  24.8 2.5 %shard_map.123 = (f32[192,2048]{1,0:T(8,128)S(1)}, bf16[16,192,192]{2,1,0:T(8,128)(2,1)S(1)}, f32[16,192,192]{2,1,0:T(8,128)S(1)}, bf16[192,2048]{1,0:T(8,128)(2,1)S(1)}, bf16[192,2048]{1,0:T(8,128)(2,1)S(1)}) custom-call(f32[32,192]{1,0:T(8,128)S(1)} %get-tuple-element.72.refs_2_.refs_0_, f32[192,2048]{1,0:T(8,128)S(1)} %get-tuple-element.74.refs_5_.refs_1_.refs_0_, ...), custom_call_target="tpu_custom_call" | custom-call | flops 301989888 | bytes 4718592 | tf_op jit(solution)/shard_map/pallas_call | solution.py:86
  27.4 3.0 %collective-permute-done.4.refs_2_.refs_6_ = bf16[528,128]{1,0:T(8,128)(2,1)S(1)} collective-permute-done((bf16[528,128]{1,0:T(8,128)(2,1)S(1)}, bf16[528,128]{1,0:T(8,128)(2,1)S(1)}, u32[]{:S(2)}, u32[]{:S(2)}) %collective-permute-start.4) | collective-permute-done | bytes 135200 | tf_op jit(solution)/shard_map/ppermute | solution.py:600
  30.4 1.4 %collective-permute-done.5.refs_3_.refs_7_ = bf16[528,128]{1,0:T(8,128)(2,1)S(1)} collective-permute-done((bf16[528,128]{1,0:T(8,128)(2,1)S(1)}, bf16[528,128]{1,0:T(8,128)(2,1)S(1)}, u32[]{:S(2)}, u32[]{:S(2)}) %collective-permute-start.5) | collective-permute-done | bytes 135200 | tf_op jit(solution)/shard_map/ppermute | solution.py:600
  31.9 0.3 shard_map.124.refs_5_
  32.1 0.0 collective-permute-done.7.refs_4_
  32.1 0.3 shard_map.125
  32.5 1.4 %collective-permute-start.8 = (bf16[512,128]{1,0:T(8,128)(2,1)S(1)}, bf16[512,128]{1,0:T(8,128)(2,1)S(1)}, u32[]{:S(2)}, u32[]{:S(2)}) collective-permute-start(bf16[512,128]{1,0:T(8,128)(2,1)S(1)} %get-tuple-element.88), channel_id=1, source_target_pairs={{0,4},{4,0},{8,12},{12,8},{16,20},{20,16},{24,28},{28,24},{1,5},{5... | collective-permute-start | bytes 393224 | tf_op jit(solution)/shard_map/ppermute | solution.py:600
  33.9 2.6 %collective-permute-start.9 = (bf16[512,128]{1,0:T(8,128)(2,1)S(1)}, bf16[512,128]{1,0:T(8,128)(2,1)S(1)}, u32[]{:S(2)}, u32[]{:S(2)}) collective-permute-start(bf16[512,128]{1,0:T(8,128)(2,1)S(1)} %get-tuple-element.89), channel_id=1, source_target_pairs={{0,8},{4,12},{8,0},{12,4},{16,24},{20,28},{24,16},{28,20},{1,9},{5... | collective-permute-start | bytes 393224 | tf_op jit(solution)/shard_map/ppermute | solution.py:600
  36.5 0.8 collective-permute-start.10
  37.3 2.9 %collective-permute-start.6 = (bf16[2,512,128]{2,1,0:T(8,128)(2,1)S(1)}, bf16[2,512,128]{2,1,0:T(8,128)(2,1)S(1)}, u32[]{:S(2)}, u32[]{:S(2)}) collective-permute-start(bf16[2,512,128]{2,1,0:T(8,128)(2,1)S(1)} %shard_map.124.refs_5_), channel_id=1, source_target_pairs={{0,16},{4,20},{8,24},{12,28},{1,17},{5,21},{9,25},{13,29},{2,18},{... | collective-permute-start | bytes 786440 | tf_op jit(solution)/shard_map/ppermute | solution.py:606
  40.2 0.0 collective-permute-done.8.refs_5_.refs_8_
  40.2 0.0 collective-permute-done.9.refs_6_.refs_9_
  40.2 2.2 %collective-permute-done.10.refs_7_.refs_10_ = bf16[512,128]{1,0:T(8,128)(2,1)S(1)} collective-permute-done((bf16[512,128]{1,0:T(8,128)(2,1)S(1)}, bf16[512,128]{1,0:T(8,128)(2,1)S(1)}, u32[]{:S(2)}, u32[]{:S(2)}) %collective-permute-start.10) | collective-permute-done | bytes 131104 | tf_op jit(solution)/shard_map/ppermute | solution.py:600
  42.4 4.7 %shard_map.126 = (bf16[192,4096]{1,0:T(8,128)(2,1)}, bf16[192,2048]{1,0:T(8,128)(2,1)S(1)}, bf16[528,128]{1,0:T(8,128)(2,1)S(1)}, bf16[528,128]{1,0:T(8,128)(2,1...) custom-call(f32[192,2048]{1,0:T(8,128)S(1)} %get-tuple-element.79.refs_4_.refs_0_, ...), custom_call_target="tpu_custom_call" | custom-call | flops 201326592 | bytes 4718592 | tf_op jit(solution)/shard_map/pallas_call | solution.py:86
  47.1 1.4 %collective-permute-start.14 = (bf16[528,128]{1,0:T(8,128)(2,1)S(1)}, bf16[528,128]{1,0:T(8,128)(2,1)S(1)}, u32[]{:S(2)}, u32[]{:S(2)}) collective-permute-start(bf16[528,128]{1,0:T(8,128)(2,1)S(1)} %get-tuple-element.98), channel_id=1, source_target_pairs={{0,4},{4,0},{8,12},{12,8},{16,20},{20,16},{24,28},{28,24},{1,5},{5... | collective-permute-start | bytes 405512 | tf_op jit(solution)/shard_map/ppermute | solution.py:600
  48.5 1.4 %collective-permute-start.15 = (bf16[528,128]{1,0:T(8,128)(2,1)S(1)}, bf16[528,128]{1,0:T(8,128)(2,1)S(1)}, u32[]{:S(2)}, u32[]{:S(2)}) collective-permute-start(bf16[528,128]{1,0:T(8,128)(2,1)S(1)} %get-tuple-element.99), channel_id=1, source_target_pairs={{0,8},{4,12},{8,0},{12,4},{16,24},{20,28},{24,16},{28,20},{1,9},{5... | collective-permute-start | bytes 405512 | tf_op jit(solution)/shard_map/ppermute | solution.py:600
  49.9 0.8 collective-permute-start.16
  50.7 0.3 shard_map.127
  51.0 1.4 %collective-permute-start.11 = (bf16[512,128]{1,0:T(8,128)(2,1)S(1)}, bf16[512,128]{1,0:T(8,128)(2,1)S(1)}, u32[]{:S(2)}, u32[]{:S(2)}) collective-permute-start(bf16[512,128]{1,0:T(8,128)(2,1)S(1)} %get-tuple-element.93), channel_id=1, source_target_pairs={{0,4},{4,0},{8,12},{12,8},{16,20},{20,16},{24,28},{28,24},{1,5},{5... | collective-permute-start | bytes 393224 | tf_op jit(solution)/shard_map/ppermute | solution.py:600
  52.4 2.0 %collective-permute-start.12 = (bf16[512,128]{1,0:T(8,128)(2,1)S(1)}, bf16[512,128]{1,0:T(8,128)(2,1)S(1)}, u32[]{:S(2)}, u32[]{:S(2)}) collective-permute-start(bf16[512,128]{1,0:T(8,128)(2,1)S(1)} %get-tuple-element.94), channel_id=1, source_target_pairs={{0,8},{4,12},{8,0},{12,4},{16,24},{20,28},{24,16},{28,20},{1,9},{5... | collective-permute-start | bytes 393224 | tf_op jit(solution)/shard_map/ppermute | solution.py:600
  54.4 0.5 collective-permute-start.13
  55.0 0.0 collective-permute-done.15.refs_2_
  55.0 2.3 %collective-permute-done.16.refs_3_ = bf16[528,128]{1,0:T(8,128)(2,1)S(1)} collective-permute-done((bf16[528,128]{1,0:T(8,128)(2,1)S(1)}, bf16[528,128]{1,0:T(8,128)(2,1)S(1)}, u32[]{:S(2)}, u32[]{:S(2)}) %collective-permute-start.16) | collective-permute-done | bytes 135200 | tf_op jit(solution)/shard_map/ppermute | solution.py:600
  57.3 0.4 shard_map.128
  57.7 1.3 %collective-permute-start.17 = (bf16[2,512,128]{2,1,0:T(8,128)(2,1)S(1)}, bf16[2,512,128]{2,1,0:T(8,128)(2,1)S(1)}, u32[]{:S(2)}, u32[]{:S(2)}) collective-permute-start(bf16[2,512,128]{2,1,0:T(8,128)(2,1)S(1)} %get-tuple-element.109), channel_id=1, source_target_pairs={{16,0},{20,4},{24,8},{28,12},{17,1},{21,5},{25,9},{29,13},{18,2},{... | collective-permute-start | bytes 786440 | tf_op jit(solution)/shard_map/ppermute | solution.py:606
  59.0 0.2 collective-permute-done.12.refs_6_.refs_9_
  59.2 2.2 %collective-permute-done.13.refs_7_.refs_10_ = bf16[512,128]{1,0:T(8,128)(2,1)S(1)} collective-permute-done((bf16[512,128]{1,0:T(8,128)(2,1)S(1)}, bf16[512,128]{1,0:T(8,128)(2,1)S(1)}, u32[]{:S(2)}, u32[]{:S(2)}) %collective-permute-start.13) | collective-permute-done | bytes 131104 | tf_op jit(solution)/shard_map/ppermute | solution.py:600
  61.4 4.8 %shard_map.129 = (bf16[192,4096]{1,0:T(8,128)(2,1)}, bf16[192,2048]{1,0:T(8,128)(2,1)S(1)}, bf16[528,128]{1,0:T(8,128)(2,1)S(1)}, bf16[528,128]{1,0:T(8,128)(2,1...) custom-call(f32[192,2048]{1,0:T(8,128)S(1)} %get-tuple-element.80.refs_4_.refs_, ...), custom_call_target="tpu_custom_call", output_to_operand_aliasing={{0}: (8, {})} | custom-call | flops 201326592 | bytes 4718592 | tf_op jit(solution)/shard_map/pallas_call | solution.py:86
  66.2 1.3 %collective-permute-start.18 = (bf16[528,128]{1,0:T(8,128)(2,1)S(1)}, bf16[528,128]{1,0:T(8,128)(2,1)S(1)}, u32[]{:S(2)}, u32[]{:S(2)}) collective-permute-start(bf16[528,128]{1,0:T(8,128)(2,1)S(1)} %get-tuple-element.111), channel_id=1, source_target_pairs={{0,4},{4,0},{8,12},{12,8},{16,20},{20,16},{24,28},{28,24},{1,5},{5... | collective-permute-start | bytes 405512 | tf_op jit(solution)/shard_map/ppermute | solution.py:600
  67.4 0.8 collective-permute-start.19
  68.3 1.5 %collective-permute-start.20 = (bf16[528,128]{1,0:T(8,128)(2,1)S(1)}, bf16[528,128]{1,0:T(8,128)(2,1)S(1)}, u32[]{:S(2)}, u32[]{:S(2)}) collective-permute-start(bf16[528,128]{1,0:T(8,128)(2,1)S(1)} %get-tuple-element.113), channel_id=1, source_target_pairs={{0,12},{4,8},{8,4},{12,0},{16,28},{20,24},{24,20},{28,16},{1,13},{... | collective-permute-start | bytes 405512 | tf_op jit(solution)/shard_map/ppermute | solution.py:600
  69.7 5.9 %shard_map.130 = (bf16[192,4096]{1,0:T(8,128)(2,1)}, f32[192,2048]{1,0:T(8,128)S(1)}, f32[192,2048]{1,0:T(8,128)S(1)}) custom-call(f32[192,2048]{1,0:T(8,128)S(1)} %get-tuple-element.73.refs_5_.refs_1_.refs_0_, f32[16,192,192]{2,1,0:T(8,128)S(1)} %get-tuple-element.106.refs_1_, bf16[192,4096]{1,0:T(8,128)(2,1)S(1)} %copy-done.2, ...), custom_call_target="tpu_custom_call" | custom-call | flops 754974720 | bytes 7864320 | tf_op jit(solution)/shard_map/pallas_call | solution.py:86
  75.6 0.0 collective-permute-done.18.refs_1_
  75.7 0.0 collective-permute-done.19.refs_2_
  75.7 2.9 %collective-permute-done.20.refs_3_ = bf16[528,128]{1,0:T(8,128)(2,1)S(1)} collective-permute-done((bf16[528,128]{1,0:T(8,128)(2,1)S(1)}, bf16[528,128]{1,0:T(8,128)(2,1)S(1)}, u32[]{:S(2)}, u32[]{:S(2)}) %collective-permute-start.20) | collective-permute-done | bytes 135200 | tf_op jit(solution)/shard_map/ppermute | solution.py:600
  78.6 0.4 shard_map.131
  79.0 1.3 %collective-permute-start.21 = (bf16[2,512,128]{2,1,0:T(8,128)(2,1)S(1)}, bf16[2,512,128]{2,1,0:T(8,128)(2,1)S(1)}, u32[]{:S(2)}, u32[]{:S(2)}) collective-permute-start(bf16[2,512,128]{2,1,0:T(8,128)(2,1)S(1)} %get-tuple-element.122), channel_id=1, source_target_pairs={{16,0},{20,4},{24,8},{28,12},{17,1},{21,5},{25,9},{29,13},{18,2},{... | collective-permute-start | bytes 786440 | tf_op jit(solution)/shard_map/ppermute | solution.py:606
  80.3 0.4 shard_map.132
  80.8 0.1 collective-permute-start.22
  80.8 0.1 collective-permute-start.23
  80.9 3.4 %collective-permute-start.24 = (bf16[544,128]{1,0:T(8,128)(2,1)S(1)}, bf16[544,128]{1,0:T(8,128)(2,1)S(1)}, u32[]{:S(2)}, u32[]{:S(2)}) collective-permute-start(bf16[544,128]{1,0:T(8,128)(2,1)S(1)} %get-tuple-element.128), channel_id=1, source_target_pairs={{0,12},{4,8},{8,4},{12,0},{16,28},{20,24},{24,20},{28,16},{1,13},{... | collective-permute-start | bytes 417800 | tf_op jit(solution)/shard_map/ppermute | solution.py:600
  84.3 5.9 %shard_map.133 = (bf16[192,4096]{1,0:T(8,128)(2,1)}, f32[192,2048]{1,0:T(8,128)S(1)}, f32[192,2048]{1,0:T(8,128)S(1)}) custom-call(f32[192,2048]{1,0:T(8,128)S(1)} %get-tuple-element.74.refs_5_.refs_1_.refs_0_, f32[16,192,192]{2,1,0:T(8,128)S(1)} %get-tuple-element.103.refs_1_, bf16[192,4096]{1,0:T(8,128)(2,1)S(1)} %copy-done.2, ...), custom_call_target="tpu_custom_call", output_to_operand_aliasing={{0}: (11, {})} | custom-call | flops 754974720 | bytes 7864320 | tf_op jit(solution)/shard_map/pallas_call | solution.py:86
  90.2 3.8 %collective-permute-done.24.refs_7_ = bf16[544,128]{1,0:T(8,128)(2,1)S(1)} collective-permute-done((bf16[544,128]{1,0:T(8,128)(2,1)S(1)}, bf16[544,128]{1,0:T(8,128)(2,1)S(1)}, u32[]{:S(2)}, u32[]{:S(2)}) %collective-permute-start.24) | collective-permute-done | bytes 139296 | tf_op jit(solution)/shard_map/ppermute | solution.py:600
  94.1 2.0 %shard_map.134 = (bf16[192,4096]{1,0:T(8,128)(2,1)}, bf16[192,4096]{1,0:T(8,128)(2,1)}, f32[32,128]{1,0:T(8,128)S(1)}) custom-call(bf16[192,2048]{1,0:T(8,128)(2,1)S(1)} %get-tuple-element.123.refs_0_, bf16[192,2048]{1,0:T(8,128)(2,1)S(1)} %get-tuple-element.124.refs_1_, f32[192,2048]{1,0:T(8,128)S(1)} %get-tuple-element.114.refs_9_.refs_2_, ...), custom_call_target="tpu_custom_call" | custom-call | flops 201326592 | bytes 6291456 | tf_op jit(solution)/shard_map/pallas_call | solution.py:86
  96.1 0.4 shard_map.135
  96.5 0.1 collective-permute-start.25
  96.6 0.1 collective-permute-start.26
  96.7 3.4 %collective-permute-start.27 = (bf16[512,128]{1,0:T(8,128)(2,1)S(1)}, bf16[512,128]{1,0:T(8,128)(2,1)S(1)}, u32[]{:S(2)}, u32[]{:S(2)}) collective-permute-start(bf16[512,128]{1,0:T(8,128)(2,1)S(1)} %get-tuple-element.133), channel_id=1, source_target_pairs={{0,12},{4,8},{8,4},{12,0},{16,28},{20,24},{24,20},{28,16},{1,13},{... | collective-permute-start | bytes 393224 | tf_op jit(solution)/shard_map/ppermute | solution.py:600
  100.1 1.6 %collective-permute-start.28 = (f32[32,128]{1,0:T(8,128)S(1)}, f32[32,128]{1,0:T(8,128)S(1)}, u32[]{:S(2)}, u32[]{:S(2)}) collective-permute-start(f32[32,128]{1,0:T(8,128)S(1)} %get-tuple-element.129.refs_9_.refs_8_), channel_id=1, source_target_pairs={{0,16},{4,20},{8,24},{12,28},{16,0},{20,4},{24,8},{28,12},{1,17},{... | collective-permute-start | bytes 49160 | tf_op jit(solution)/shard_map/ppermute | solution.py:644
  101.7 3.1 %collective-permute-done.28.refs_9_ = f32[32,128]{1,0:T(8,128)S(1)} collective-permute-done((f32[32,128]{1,0:T(8,128)S(1)}, f32[32,128]{1,0:T(8,128)S(1)}, u32[]{:S(2)}, u32[]{:S(2)}) %collective-permute-start.28) | collective-permute-done | bytes 16416 | tf_op jit(solution)/shard_map/ppermute | solution.py:644
  104.7 2.6 %shard_map.136 = (bf16[192,4096]{1,0:T(8,128)(2,1)}, bf16[192,4096]{1,0:T(8,128)(2,1)}, f32[32,128]{1,0:T(8,128)}) custom-call(bf16[192,2048]{1,0:T(8,128)(2,1)S(1)} %get-tuple-element.118.refs_0_, bf16[192,2048]{1,0:T(8,128)(2,1)S(1)} %get-tuple-element.119.refs_1_, ...), custom_call_target="tpu_custom_call", output_to_operand_aliasing={{0}: (10, {}), {1}: (11, {})} | custom-call | flops 201326592 | bytes 6291456 | tf_op jit(solution)/shard_map/pallas_call | solution.py:86
  (22 shorter events, 0.0 us)
Async XLA Ops:
  5.5 10.4 %collective-permute-start = (bf16[528,128]{1,0:T(8,128)(2,1)S(1)}, bf16[528,128]{1,0:T(8,128)(2,1)S(1)}, u32[]{:S(2)}, u32[]{:S(2)}) collective-permute-start(bf16[528,128]{1,0:T(8,128)(2,1)S(1)} %get-tuple-element.76), channel_id=1, source_target_pairs={{0,4},{4,0},{8,12},{12,8},{16,20},{20,16},{24,28},{28,24},{1,5},{5... | collective-permute-start | bytes 405512 | tf_op jit(solution)/shard_map/ppermute | solution.py:600
  8.6 7.4 %collective-permute-start.1 = (bf16[528,128]{1,0:T(8,128)(2,1)S(1)}, bf16[528,128]{1,0:T(8,128)(2,1)S(1)}, u32[]{:S(2)}, u32[]{:S(2)}) collective-permute-start(bf16[528,128]{1,0:T(8,128)(2,1)S(1)} %get-tuple-element.77), channel_id=1, source_target_pairs={{0,8},{4,12},{8,0},{12,4},{16,24},{20,28},{24,16},{28,20},{1,9},{5... | collective-permute-start | bytes 405512 | tf_op jit(solution)/shard_map/ppermute | solution.py:600
  10.2 6.2 %collective-permute-start.2 = (bf16[528,128]{1,0:T(8,128)(2,1)S(1)}, bf16[528,128]{1,0:T(8,128)(2,1)S(1)}, u32[]{:S(2)}, u32[]{:S(2)}) collective-permute-start(bf16[528,128]{1,0:T(8,128)(2,1)S(1)} %get-tuple-element.78), channel_id=1, source_target_pairs={{0,12},{4,8},{8,4},{12,0},{16,28},{20,24},{24,20},{28,16},{1,13},{... | collective-permute-start | bytes 405512 | tf_op jit(solution)/shard_map/ppermute | solution.py:600
  10.2 3.2 %copy-start = (bf16[192,4096]{1,0:T(8,128)(2,1)S(1)}, bf16[192,4096]{1,0:T(8,128)(2,1)}, u32[]{:S(2)}) copy-start(bf16[192,4096]{1,0:T(8,128)(2,1)} %refs_3_.11) | copy-start | bytes 4718596
  10.2 3.2 %copy-start.1 = (bf16[192,4096]{1,0:T(8,128)(2,1)S(1)}, bf16[192,4096]{1,0:T(8,128)(2,1)}, u32[]{:S(2)}) copy-start(bf16[192,4096]{1,0:T(8,128)(2,1)} %refs_4_.11) | copy-start | bytes 4718596
  10.2 3.2 %copy-start.2 = (bf16[192,4096]{1,0:T(8,128)(2,1)S(1)}, bf16[192,4096]{1,0:T(8,128)(2,1)}, u32[]{:S(2)}) copy-start(bf16[192,4096]{1,0:T(8,128)(2,1)} %refs_2_.11) | copy-start | bytes 4718596
  16.6 15.5 %collective-permute-start.7 = (bf16[2,512,128]{2,1,0:T(8,128)(2,1)S(1)}, bf16[2,512,128]{2,1,0:T(8,128)(2,1)S(1)}, u32[]{:S(2)}, u32[]{:S(2)}) collective-permute-start(bf16[2,512,128]{2,1,0:T(8,128)(2,1)S(1)} %shard_map.122.refs_5_), channel_id=1, source_target_pairs={{0,16},{4,20},{8,24},{12,28},{1,17},{5,21},{9,25},{13,29},{2,18},{... | collective-permute-start | bytes 786440 | tf_op jit(solution)/shard_map/ppermute | solution.py:606
  21.3 6.1 %collective-permute-start.3 = (bf16[528,128]{1,0:T(8,128)(2,1)S(1)}, bf16[528,128]{1,0:T(8,128)(2,1)S(1)}, u32[]{:S(2)}, u32[]{:S(2)}) collective-permute-start(bf16[528,128]{1,0:T(8,128)(2,1)S(1)} %get-tuple-element.83), channel_id=1, source_target_pairs={{0,4},{4,0},{8,12},{12,8},{16,20},{20,16},{24,28},{28,24},{1,5},{5... | collective-permute-start | bytes 405512 | tf_op jit(solution)/shard_map/ppermute | solution.py:600
  22.8 7.6 %collective-permute-start.4 = (bf16[528,128]{1,0:T(8,128)(2,1)S(1)}, bf16[528,128]{1,0:T(8,128)(2,1)S(1)}, u32[]{:S(2)}, u32[]{:S(2)}) collective-permute-start(bf16[528,128]{1,0:T(8,128)(2,1)S(1)} %get-tuple-element.84), channel_id=1, source_target_pairs={{0,8},{4,12},{8,0},{12,4},{16,24},{20,28},{24,16},{28,20},{1,9},{5... | collective-permute-start | bytes 405512 | tf_op jit(solution)/shard_map/ppermute | solution.py:600
  24.4 7.4 %collective-permute-start.5 = (bf16[528,128]{1,0:T(8,128)(2,1)S(1)}, bf16[528,128]{1,0:T(8,128)(2,1)S(1)}, u32[]{:S(2)}, u32[]{:S(2)}) collective-permute-start(bf16[528,128]{1,0:T(8,128)(2,1)S(1)} %get-tuple-element.85), channel_id=1, source_target_pairs={{0,12},{4,8},{8,4},{12,0},{16,28},{20,24},{24,20},{28,16},{1,13},{... | collective-permute-start | bytes 405512 | tf_op jit(solution)/shard_map/ppermute | solution.py:600
  31.9 10.5 %copy-start.3 = (bf16[192,4096]{1,0:T(8,128)(2,1)S(1)}, bf16[192,4096]{1,0:T(8,128)(2,1)}, u32[]{:S(2)}) copy-start(bf16[192,4096]{1,0:T(8,128)(2,1)} %refs_2_.9) | copy-start | bytes 4718596
  31.9 10.5 %copy-start.4 = (f32[4096]{0:T(1024)S(1)}, f32[4096]{0:T(1024)}, u32[]{:S(2)}) copy-start(f32[4096]{0:T(1024)} %param.13) | copy-start | bytes 49156
  32.5 7.7 %collective-permute-start.8 = (bf16[512,128]{1,0:T(8,128)(2,1)S(1)}, bf16[512,128]{1,0:T(8,128)(2,1)S(1)}, u32[]{:S(2)}, u32[]{:S(2)}) collective-permute-start(bf16[512,128]{1,0:T(8,128)(2,1)S(1)} %get-tuple-element.88), channel_id=1, source_target_pairs={{0,4},{4,0},{8,12},{12,8},{16,20},{20,16},{24,28},{28,24},{1,5},{5... | collective-permute-start | bytes 393224 | tf_op jit(solution)/shard_map/ppermute | solution.py:600
  33.9 6.3 %collective-permute-start.9 = (bf16[512,128]{1,0:T(8,128)(2,1)S(1)}, bf16[512,128]{1,0:T(8,128)(2,1)S(1)}, u32[]{:S(2)}, u32[]{:S(2)}) collective-permute-start(bf16[512,128]{1,0:T(8,128)(2,1)S(1)} %get-tuple-element.89), channel_id=1, source_target_pairs={{0,8},{4,12},{8,0},{12,4},{16,24},{20,28},{24,16},{28,20},{1,9},{5... | collective-permute-start | bytes 393224 | tf_op jit(solution)/shard_map/ppermute | solution.py:600
  36.5 5.9 %collective-permute-start.10 = (bf16[512,128]{1,0:T(8,128)(2,1)S(1)}, bf16[512,128]{1,0:T(8,128)(2,1)S(1)}, u32[]{:S(2)}, u32[]{:S(2)}) collective-permute-start(bf16[512,128]{1,0:T(8,128)(2,1)S(1)} %get-tuple-element.90), channel_id=1, source_target_pairs={{0,12},{4,8},{8,4},{12,0},{16,28},{20,24},{24,20},{28,16},{1,13},{... | collective-permute-start | bytes 393224 | tf_op jit(solution)/shard_map/ppermute | solution.py:600
  37.3 13.4 %collective-permute-start.6 = (bf16[2,512,128]{2,1,0:T(8,128)(2,1)S(1)}, bf16[2,512,128]{2,1,0:T(8,128)(2,1)S(1)}, u32[]{:S(2)}, u32[]{:S(2)}) collective-permute-start(bf16[2,512,128]{2,1,0:T(8,128)(2,1)S(1)} %shard_map.124.refs_5_), channel_id=1, source_target_pairs={{0,16},{4,20},{8,24},{12,28},{1,17},{5,21},{9,25},{13,29},{2,18},{... | collective-permute-start | bytes 786440 | tf_op jit(solution)/shard_map/ppermute | solution.py:606
  47.1 7.3 %collective-permute-start.14 = (bf16[528,128]{1,0:T(8,128)(2,1)S(1)}, bf16[528,128]{1,0:T(8,128)(2,1)S(1)}, u32[]{:S(2)}, u32[]{:S(2)}) collective-permute-start(bf16[528,128]{1,0:T(8,128)(2,1)S(1)} %get-tuple-element.98), channel_id=1, source_target_pairs={{0,4},{4,0},{8,12},{12,8},{16,20},{20,16},{24,28},{28,24},{1,5},{5... | collective-permute-start | bytes 405512 | tf_op jit(solution)/shard_map/ppermute | solution.py:600
  48.5 6.5 %collective-permute-start.15 = (bf16[528,128]{1,0:T(8,128)(2,1)S(1)}, bf16[528,128]{1,0:T(8,128)(2,1)S(1)}, u32[]{:S(2)}, u32[]{:S(2)}) collective-permute-start(bf16[528,128]{1,0:T(8,128)(2,1)S(1)} %get-tuple-element.99), channel_id=1, source_target_pairs={{0,8},{4,12},{8,0},{12,4},{16,24},{20,28},{24,16},{28,20},{1,9},{5... | collective-permute-start | bytes 405512 | tf_op jit(solution)/shard_map/ppermute | solution.py:600
  49.9 7.4 %collective-permute-start.16 = (bf16[528,128]{1,0:T(8,128)(2,1)S(1)}, bf16[528,128]{1,0:T(8,128)(2,1)S(1)}, u32[]{:S(2)}, u32[]{:S(2)}) collective-permute-start(bf16[528,128]{1,0:T(8,128)(2,1)S(1)} %get-tuple-element.100), channel_id=1, source_target_pairs={{0,12},{4,8},{8,4},{12,0},{16,28},{20,24},{24,20},{28,16},{1,13},{... | collective-permute-start | bytes 405512 | tf_op jit(solution)/shard_map/ppermute | solution.py:600
  51.0 8.0 %collective-permute-start.11 = (bf16[512,128]{1,0:T(8,128)(2,1)S(1)}, bf16[512,128]{1,0:T(8,128)(2,1)S(1)}, u32[]{:S(2)}, u32[]{:S(2)}) collective-permute-start(bf16[512,128]{1,0:T(8,128)(2,1)S(1)} %get-tuple-element.93), channel_id=1, source_target_pairs={{0,4},{4,0},{8,12},{12,8},{16,20},{20,16},{24,28},{28,24},{1,5},{5... | collective-permute-start | bytes 393224 | tf_op jit(solution)/shard_map/ppermute | solution.py:600
  52.4 6.8 %collective-permute-start.12 = (bf16[512,128]{1,0:T(8,128)(2,1)S(1)}, bf16[512,128]{1,0:T(8,128)(2,1)S(1)}, u32[]{:S(2)}, u32[]{:S(2)}) collective-permute-start(bf16[512,128]{1,0:T(8,128)(2,1)S(1)} %get-tuple-element.94), channel_id=1, source_target_pairs={{0,8},{4,12},{8,0},{12,4},{16,24},{20,28},{24,16},{28,20},{1,9},{5... | collective-permute-start | bytes 393224 | tf_op jit(solution)/shard_map/ppermute | solution.py:600
  54.4 7.0 %collective-permute-start.13 = (bf16[512,128]{1,0:T(8,128)(2,1)S(1)}, bf16[512,128]{1,0:T(8,128)(2,1)S(1)}, u32[]{:S(2)}, u32[]{:S(2)}) collective-permute-start(bf16[512,128]{1,0:T(8,128)(2,1)S(1)} %get-tuple-element.95), channel_id=1, source_target_pairs={{0,12},{4,8},{8,4},{12,0},{16,28},{20,24},{24,20},{28,16},{1,13},{... | collective-permute-start | bytes 393224 | tf_op jit(solution)/shard_map/ppermute | solution.py:600
  57.7 22.6 %collective-permute-start.17 = (bf16[2,512,128]{2,1,0:T(8,128)(2,1)S(1)}, bf16[2,512,128]{2,1,0:T(8,128)(2,1)S(1)}, u32[]{:S(2)}, u32[]{:S(2)}) collective-permute-start(bf16[2,512,128]{2,1,0:T(8,128)(2,1)S(1)} %get-tuple-element.109), channel_id=1, source_target_pairs={{16,0},{20,4},{24,8},{28,12},{17,1},{21,5},{25,9},{29,13},{18,2},{... | collective-permute-start | bytes 786440 | tf_op jit(solution)/shard_map/ppermute | solution.py:606
  66.2 9.5 %collective-permute-start.18 = (bf16[528,128]{1,0:T(8,128)(2,1)S(1)}, bf16[528,128]{1,0:T(8,128)(2,1)S(1)}, u32[]{:S(2)}, u32[]{:S(2)}) collective-permute-start(bf16[528,128]{1,0:T(8,128)(2,1)S(1)} %get-tuple-element.111), channel_id=1, source_target_pairs={{0,4},{4,0},{8,12},{12,8},{16,20},{20,16},{24,28},{28,24},{1,5},{5... | collective-permute-start | bytes 405512 | tf_op jit(solution)/shard_map/ppermute | solution.py:600
  67.4 8.2 %collective-permute-start.19 = (bf16[528,128]{1,0:T(8,128)(2,1)S(1)}, bf16[528,128]{1,0:T(8,128)(2,1)S(1)}, u32[]{:S(2)}, u32[]{:S(2)}) collective-permute-start(bf16[528,128]{1,0:T(8,128)(2,1)S(1)} %get-tuple-element.112), channel_id=1, source_target_pairs={{0,8},{4,12},{8,0},{12,4},{16,24},{20,28},{24,16},{28,20},{1,9},{5... | collective-permute-start | bytes 405512 | tf_op jit(solution)/shard_map/ppermute | solution.py:600
  68.3 10.4 %collective-permute-start.20 = (bf16[528,128]{1,0:T(8,128)(2,1)S(1)}, bf16[528,128]{1,0:T(8,128)(2,1)S(1)}, u32[]{:S(2)}, u32[]{:S(2)}) collective-permute-start(bf16[528,128]{1,0:T(8,128)(2,1)S(1)} %get-tuple-element.113), channel_id=1, source_target_pairs={{0,12},{4,8},{8,4},{12,0},{16,28},{20,24},{24,20},{28,16},{1,13},{... | collective-permute-start | bytes 405512 | tf_op jit(solution)/shard_map/ppermute | solution.py:600
  79.0 17.1 %collective-permute-start.21 = (bf16[2,512,128]{2,1,0:T(8,128)(2,1)S(1)}, bf16[2,512,128]{2,1,0:T(8,128)(2,1)S(1)}, u32[]{:S(2)}, u32[]{:S(2)}) collective-permute-start(bf16[2,512,128]{2,1,0:T(8,128)(2,1)S(1)} %get-tuple-element.122), channel_id=1, source_target_pairs={{16,0},{20,4},{24,8},{28,12},{17,1},{21,5},{25,9},{29,13},{18,2},{... | collective-permute-start | bytes 786440 | tf_op jit(solution)/shard_map/ppermute | solution.py:606
  80.8 9.5 %collective-permute-start.22 = (bf16[544,128]{1,0:T(8,128)(2,1)S(1)}, bf16[544,128]{1,0:T(8,128)(2,1)S(1)}, u32[]{:S(2)}, u32[]{:S(2)}) collective-permute-start(bf16[544,128]{1,0:T(8,128)(2,1)S(1)} %get-tuple-element.126), channel_id=1, source_target_pairs={{0,4},{4,0},{8,12},{12,8},{16,20},{20,16},{24,28},{28,24},{1,5},{5... | collective-permute-start | bytes 417800 | tf_op jit(solution)/shard_map/ppermute | solution.py:600
  80.8 9.4 %collective-permute-start.23 = (bf16[544,128]{1,0:T(8,128)(2,1)S(1)}, bf16[544,128]{1,0:T(8,128)(2,1)S(1)}, u32[]{:S(2)}, u32[]{:S(2)}) collective-permute-start(bf16[544,128]{1,0:T(8,128)(2,1)S(1)} %get-tuple-element.127), channel_id=1, source_target_pairs={{0,8},{4,12},{8,0},{12,4},{16,24},{20,28},{24,16},{28,20},{1,9},{5... | collective-permute-start | bytes 417800 | tf_op jit(solution)/shard_map/ppermute | solution.py:600
  80.9 13.2 %collective-permute-start.24 = (bf16[544,128]{1,0:T(8,128)(2,1)S(1)}, bf16[544,128]{1,0:T(8,128)(2,1)S(1)}, u32[]{:S(2)}, u32[]{:S(2)}) collective-permute-start(bf16[544,128]{1,0:T(8,128)(2,1)S(1)} %get-tuple-element.128), channel_id=1, source_target_pairs={{0,12},{4,8},{8,4},{12,0},{16,28},{20,24},{24,20},{28,16},{1,13},{... | collective-permute-start | bytes 417800 | tf_op jit(solution)/shard_map/ppermute | solution.py:600
  96.5 8.2 %collective-permute-start.25 = (bf16[512,128]{1,0:T(8,128)(2,1)S(1)}, bf16[512,128]{1,0:T(8,128)(2,1)S(1)}, u32[]{:S(2)}, u32[]{:S(2)}) collective-permute-start(bf16[512,128]{1,0:T(8,128)(2,1)S(1)} %get-tuple-element.131), channel_id=1, source_target_pairs={{0,4},{4,0},{8,12},{12,8},{16,20},{20,16},{24,28},{28,24},{1,5},{5... | collective-permute-start | bytes 393224 | tf_op jit(solution)/shard_map/ppermute | solution.py:600
  96.6 8.1 %collective-permute-start.26 = (bf16[512,128]{1,0:T(8,128)(2,1)S(1)}, bf16[512,128]{1,0:T(8,128)(2,1)S(1)}, u32[]{:S(2)}, u32[]{:S(2)}) collective-permute-start(bf16[512,128]{1,0:T(8,128)(2,1)S(1)} %get-tuple-element.132), channel_id=1, source_target_pairs={{0,8},{4,12},{8,0},{12,4},{16,24},{20,28},{24,16},{28,20},{1,9},{5... | collective-permute-start | bytes 393224 | tf_op jit(solution)/shard_map/ppermute | solution.py:600
  96.7 8.0 %collective-permute-start.27 = (bf16[512,128]{1,0:T(8,128)(2,1)S(1)}, bf16[512,128]{1,0:T(8,128)(2,1)S(1)}, u32[]{:S(2)}, u32[]{:S(2)}) collective-permute-start(bf16[512,128]{1,0:T(8,128)(2,1)S(1)} %get-tuple-element.133), channel_id=1, source_target_pairs={{0,12},{4,8},{8,4},{12,0},{16,28},{20,24},{24,20},{28,16},{1,13},{... | collective-permute-start | bytes 393224 | tf_op jit(solution)/shard_map/ppermute | solution.py:600
  100.1 4.6 %collective-permute-start.28 = (f32[32,128]{1,0:T(8,128)S(1)}, f32[32,128]{1,0:T(8,128)S(1)}, u32[]{:S(2)}, u32[]{:S(2)}) collective-permute-start(f32[32,128]{1,0:T(8,128)S(1)} %get-tuple-element.129.refs_9_.refs_8_), channel_id=1, source_target_pairs={{0,16},{4,20},{8,24},{12,28},{16,0},{20,4},{24,8},{28,12},{1,17},{... | collective-permute-start | bytes 49160 | tf_op jit(solution)/shard_map/ppermute | solution.py:644
